TPU v7x, 128 devices: a whole 4x4x4 slice. The times are simulated.
128 devices in a mesh: dp: 8 (over y, z_hi), mp: 16 (over z_lo, x, core).
Axes of the slice: x: 4, y: 4, z: 4 (z_hi: 2, z_lo: 2; z = z_hi * 2 + z_lo), core: 2. Of those that a mesh axis runs over, the one named last changes fastest.
Arguments:
- context: bfloat16 [512, 8192], P('dp', 'mp'), may hold values from -6 to 6
- attn_weight: bfloat16 [8192, 5120], P('mp', 'dp'), may hold values from -0.0625 to 0.0625
- stream: bfloat16 [512, 5120], P(('dp', 'mp')), may hold values from -6 to 6
- norm_gain: float32 [5120], replicated, may hold values from 0.1 to 1.9
- router_weight: bfloat16 [16, 5120], replicated, may hold values from -0.078125 to 0.078125
- expert_weights: bfloat16 [16, 3, 1536, 5120], P('mp', None, 'dp'), may hold values from -0.078125 to 0.078125
- inference_slot: int32 [16], replicated, may hold values from 0 to 15, each once
- routes: int32 [512, 6], P(('dp', 'mp')), may hold values from 0 to 15, all different within a row; in each aligned block of 4 rows (0 to 3, 4 to 7, ...) at most 2 rows name the same one
Outputs:
- hidden_out: bfloat16 [512, 5120], P(('dp', 'mp'))
- expert_mix: bfloat16 [512, 5120], P(('dp', 'mp'))
- placed_experts: bfloat16 [16, 3, 1536, 5120], P(None, None, ('dp', 'mp'))
Inputs may be any that keep to these rules, and one draw needn't show every extreme that they name: inference_slot names each position once. `routes`: each row names 6 different experts. Within the rows of one device no expert is named by more than 2 rows, and in every draw some device names some expert exactly 2 times.
All inputs are finite; a program needn't handle non-finite values.
Results may differ from a plain program's by a relative error of at most 0.015.
Values may be sent and summed in bfloat16 or wider, within the bound.
No kernel may reach another device: no remote copies, remote signals or barrier semaphores. Data moves between devices by JAX's collectives and lax.ppermute only.
A program may use at most 128 MiB of HBM per device.

v0:
```python
import functools

import jax
import jax.numpy as jnp
from jax import lax
from jax.experimental import pallas as pl
from jax.experimental.pallas import tpu as pltpu
from jax.sharding import PartitionSpec as P


Z_LO, CHIPS_X, CORES = 2, 4, 2
CHIPS_Y, Z_HI = 4, 2
EARLY = 3
SHIFTS = ((0, 1), (0, 3), (1, 0), (0, 2), (1, 1), (1, 3), (1, 2))


def chip_pairs(dz, dx):
    pairs = []
    for i in range(Z_LO * CHIPS_X * CORES):
        z, x, core = i // (CHIPS_X * CORES), (i // CORES) % CHIPS_X, i % CORES
        to = (((z + dz) % Z_LO) * CHIPS_X + (x + dx) % CHIPS_X) * CORES + core
        pairs.append((i, to))
    return pairs


CORE_PAIRS = [(i, i ^ 1) for i in range(Z_LO * CHIPS_X * CORES)]


def placing_kernel(count, meta, chooser, *refs):
    blocks, out = refs[:count], refs[count]
    held, ready, in_sem, out_sem = refs[count + 1 :]
    parts, rows, slots, width = ready.shape
    lead = pl.multiple_of(8 * lax.rem(meta[0], CORES), 8)
    copies = []
    for part in range(parts):
        for k in range(count):
            ref = blocks[k].at[part, pl.ds(lead, 16), :]
            copies.append(pltpu.make_async_copy(ref, held.at[part, k], in_sem.at[part, k]))
    for copy in copies:
        copy.start()
    outward = [
        pltpu.make_async_copy(ready.at[part], out.at[part], out_sem.at[part])
        for part in range(parts)
    ]
    chunk = 1024
    for part in range(parts):
        for copy in copies[part * count : (part + 1) * count]:
            copy.wait()

        def step(at, carry, part=part):
            columns = pl.ds(pl.multiple_of(at * chunk, chunk), chunk)
            block = held[part, :, :, columns].reshape(count * 16, chunk)
            picked = jnp.dot(chooser[...], block, preferred_element_type=jnp.float32)
            ready[part, :, :, columns] = picked.astype(ready.dtype).reshape(rows, slots, chunk)
            return carry

        lax.fori_loop(0, width // chunk, step, 0)
        outward[part].start()
    for copy in outward:
        copy.wait()


def placed_blocks(me, inference_slot, blocks):
    slots = len(blocks)
    parts, rows, width = blocks[0].shape
    rows = rows // CORES
    core, chip = me % CORES, me // CORES
    z, x = chip // CHIPS_X, chip % CHIPS_X
    came = []
    for core_from in (core, 1 - core):
        for dz, dx in ((0, 0),) + SHIFTS:
            chip_from = ((z + Z_LO - dz) % Z_LO) * CHIPS_X + (x + CHIPS_X - dx) % CHIPS_X
            came.append(chip_from * CORES + core_from)
    came = jnp.stack(came)
    ids = jnp.arange(slots, dtype=jnp.int32)
    goes = jnp.sum(jnp.where(came[:, None] == ids[None, :], inference_slot[None, :], 0), axis=1)
    chooser = (
        (jnp.arange(rows)[:, None, None, None] + 4 * core == jnp.arange(16)[None, None, None, :])
        & (ids[None, :, None, None] == goes[None, None, :, None])
    ).astype(blocks[0].dtype).reshape(rows * slots, slots * 16)
    any_space = pl.BlockSpec(memory_space=pl.ANY)
    placed = pl.pallas_call(
        functools.partial(placing_kernel, slots),
        out_shape=jax.ShapeDtypeStruct((parts, rows, slots, width), blocks[0].dtype),
        in_specs=[
            pl.BlockSpec(memory_space=pltpu.SMEM),
            pl.BlockSpec(memory_space=pltpu.VMEM),
        ]
        + [any_space] * slots,
        out_specs=pl.BlockSpec(memory_space=pltpu.HBM),
        scratch_shapes=[
            pltpu.VMEM((parts, slots, 16, width), blocks[0].dtype),
            pltpu.VMEM((parts, rows, slots, width), blocks[0].dtype),
            pltpu.SemaphoreType.DMA((parts, slots)),
            pltpu.SemaphoreType.DMA((parts,)),
        ],
        compiler_params=pltpu.CompilerParams(vmem_limit_bytes=16 << 20),
        cost_estimate=pl.CostEstimate(flops=2 << 30, bytes_accessed=16 << 20, transcendentals=0),
        name="placing",
    )(me[None].astype(jnp.int32), chooser, *blocks)
    return jnp.transpose(placed, (2, 0, 1, 3))


def copy_kernel(source, out):
    out[...] = source[...]


def passed_on(array):
    shape = array.shape
    array = array.reshape(-1, shape[-1])
    return pl.pallas_call(
        copy_kernel,
        out_shape=jax.ShapeDtypeStruct(array.shape, array.dtype),
        in_specs=[pl.BlockSpec(memory_space=pltpu.VMEM)],
        out_specs=pl.BlockSpec(memory_space=pltpu.VMEM),
    )(array).reshape(shape)


def chip_slice(own, chip, rows):
    return lax.dynamic_slice_in_dim(own, chip * rows, rows, axis=1)


def moved_experts(own, inference_slot):
    me = lax.axis_index("mp")
    chip = me // CORES
    z, x = chip // CHIPS_X, chip % CHIPS_X
    chips = Z_LO * CHIPS_X
    rows = own.shape[1] // chips
    sent = []
    for dz, dx in SHIFTS:
        to = ((z + dz) % Z_LO) * CHIPS_X + (x + dx) % CHIPS_X
        sent.append(chip_slice(own, to, rows))
    sent = lax.optimization_barrier(sent[:EARLY]) + lax.optimization_barrier(sent[EARLY:])
    blocks = []
    for shift, block in zip(SHIFTS, sent):
        blocks.append(lax.ppermute(block, "mp", chip_pairs(*shift)))
    mine = chip_slice(own, chip, rows)
    swapped = []
    for block in [mine] + blocks:
        swapped.append(lax.ppermute(block, "mp", CORE_PAIRS))
    me = passed_on(me[None].astype(jnp.int32))[0]
    return placed_blocks(me, inference_slot, [mine] + blocks + swapped)


def expert_kernel(count, *refs):
    blocks, weights, outs = refs[:count], refs[count], refs[count + 1 : 2 * count + 1]
    rows_in, held, ready, row_sem, weight_sem, out_sem = refs[2 * count + 1 :]
    block_rows = blocks[0].shape[0]
    width = rows_in.shape[1]
    arrive = [
        pltpu.make_async_copy(
            blocks[n], rows_in.at[pl.ds(n * block_rows, block_rows), :], row_sem.at[n]
        )
        for n in range(count)
    ]
    fetch = [
        pltpu.make_async_copy(weights.at[part], held.at[part], weight_sem.at[part])
        for part in range(3)
    ]
    for copy in arrive + fetch:
        copy.start()
    for copy in arrive:
        copy.wait()
    contract = (((1,), (1,)), ((), ()))
    sums = []
    for part in range(2):
        fetch[part].wait()
        sums.append(
            lax.dot_general(
                rows_in[...], held[part], contract, preferred_element_type=jnp.float32
            )
        )
    opened, scale = sums
    active = (opened / (1.0 + jnp.exp(-opened)) * scale).astype(jnp.bfloat16)
    fetch[2].wait()
    chunk = 1024
    outward = []
    for at in range(width // chunk):
        columns = pl.ds(at * chunk, chunk)
        ready[:, columns] = jnp.dot(
            active, held[2, :, columns], preferred_element_type=jnp.float32
        ).astype(jnp.bfloat16)
        for n in range(count):
            copy = pltpu.make_async_copy(
                ready.at[pl.ds(n * block_rows, block_rows), columns],
                outs[n].at[:, columns],
                out_sem.at[at, n],
            )
            copy.start()
            outward.append(copy)
    for copy in outward:
        copy.wait()


def expert_apply(blocks, weights):
    count = len(blocks)
    block_rows, width = blocks[0].shape
    total = count * block_rows
    any_space = pl.BlockSpec(memory_space=pl.ANY)
    in_hbm = pl.BlockSpec(memory_space=pltpu.HBM)
    return pl.pallas_call(
        functools.partial(expert_kernel, count),
        out_shape=[jax.ShapeDtypeStruct((block_rows, width), jnp.bfloat16)] * count,
        in_specs=[any_space] * count + [in_hbm],
        out_specs=[in_hbm] * count,
        scratch_shapes=[
            pltpu.VMEM((total, width), jnp.bfloat16),
            pltpu.VMEM(weights.shape, jnp.bfloat16),
            pltpu.VMEM((total, width), jnp.bfloat16),
            pltpu.SemaphoreType.DMA((count,)),
            pltpu.SemaphoreType.DMA((3,)),
            pltpu.SemaphoreType.DMA((width // 1024, count)),
        ],
        compiler_params=pltpu.CompilerParams(vmem_limit_bytes=16 << 20),
        cost_estimate=pl.CostEstimate(flops=4 << 30, bytes_accessed=12 << 20, transcendentals=0),
        name="experts",
    )(*blocks, weights)


def row_pairs(dy, dz):
    return [(d, (d // Z_HI + dy) % CHIPS_Y * Z_HI + (d + dz) % Z_HI) for d in range(CHIPS_Y * Z_HI)]


TURNS_Y = (1, 3, 2)


def rows_of_all(own):
    other = lax.ppermute(own, "dp", row_pairs(0, 1))
    groups = []
    for block in (own, other):
        groups.append([block])
        for dy in TURNS_Y:
            groups[-1].append(lax.ppermute(block, "dp", row_pairs(dy, 0)))
    return groups[0] + groups[1]


def added(blocks):
    total = blocks[0].astype(jnp.float32)
    for block in blocks[1:]:
        total = total + block.astype(jnp.float32)
    return total.astype(jnp.bfloat16)


def sums_at_owner(partials):
    half = len(partials) // 2
    sums = []
    for turn in (1, 0):
        blocks = partials[turn * half : (turn + 1) * half]
        came = [blocks[0]]
        for dy, block in zip(TURNS_Y, blocks[1:]):
            came.append(lax.ppermute(block, "dp", row_pairs(-dy, 0)))
        if turn:
            sums.append(lax.ppermute(added(came), "dp", row_pairs(0, 1)))
        else:
            sums += came
    return added(sums)


def handoff(
    context, attn_weight, stream, norm_gain, router_weight, expert_weights, inference_slot, routes
):
    mp_count = lax.axis_size("mp")
    dp_count = lax.axis_size("dp")
    row_count = stream.shape[0]
    model_width = stream.shape[1]
    top_count = routes.shape[1]
    capacity = 2
    expert_ids = jnp.arange(mp_count, dtype=jnp.int32)
    source = jnp.sum(
        jnp.where(inference_slot[:, None] == expert_ids[None, :], expert_ids[:, None], 0), axis=0
    )
    inference_slot = passed_on(inference_slot[None])[0]
    routes = passed_on(routes)
    placed = moved_experts(expert_weights[0], inference_slot)
    column_width = attn_weight.shape[1]
    gathered = lax.all_to_all(
        jnp.broadcast_to(context[None], (dp_count, *context.shape)), "dp", 0, 0, tiled=True
    )
    partial_value = jnp.dot(
        gathered.reshape(-1, context.shape[1]), attn_weight, preferred_element_type=jnp.float32
    ).astype(jnp.bfloat16)
    partial_value = partial_value.reshape(dp_count * mp_count, row_count, column_width)
    summed = lax.all_to_all(partial_value, ("dp", "mp"), 0, 0, tiled=True)
    summed = summed.reshape(dp_count, mp_count, row_count, column_width)
    attended = jnp.sum(summed, axis=1, dtype=jnp.float32)
    attended = jnp.moveaxis(attended, 0, 1).reshape(row_count, model_width)
    hidden = (stream.astype(jnp.float32) + attended).astype(jnp.bfloat16)
    widened = hidden.astype(jnp.float32)
    normed = (
        widened * lax.rsqrt(jnp.mean(widened * widened, axis=1, keepdims=True) + 1e-06) * norm_gain
    ).astype(jnp.bfloat16)
    logits = lax.dot_general(
        normed, router_weight, (((1,), (1,)), ((), ())), preferred_element_type=jnp.float32
    )
    scores = jax.nn.sigmoid(logits)
    matches = routes[:, :, None] == expert_ids[None, None, :]
    chosen = jnp.sum(jnp.where(matches, scores[:, None, :], 0.0), axis=2)
    share = 2.5 * chosen / jnp.sum(chosen, axis=1, keepdims=True)
    destination = jnp.sum(jnp.where(matches, source[None, None, :], 0), axis=2).reshape(-1)
    onehot = (destination[:, None] == expert_ids[None, :]).astype(jnp.int32)
    earlier = jnp.cumsum(onehot, axis=0) - onehot
    position = jnp.sum(earlier * onehot, axis=1)
    slot_index = destination * capacity + position
    slot_ids = jnp.arange(mp_count * capacity, dtype=jnp.int32)
    placing = (slot_index[:, None] == slot_ids[None, :]).astype(jnp.float32)
    row_ids = jnp.arange(row_count * top_count, dtype=jnp.int32) // top_count
    row_owner = (row_ids[:, None] == jnp.arange(row_count, dtype=jnp.int32)[None, :]).astype(
        jnp.float32
    )
    pick_matrix = jnp.dot(placing.T, row_owner, precision=lax.Precision.HIGHEST).astype(
        jnp.bfloat16
    )
    outgoing = jnp.dot(pick_matrix, normed, preferred_element_type=jnp.float32).astype(jnp.bfloat16)
    outgoing = outgoing.reshape(mp_count, capacity, model_width)
    combine_matrix = jnp.dot(
        row_owner.T, placing * share.reshape(-1)[:, None], precision=lax.Precision.HIGHEST
    )
    own_rows = lax.all_to_all(outgoing, "mp", split_axis=0, concat_axis=0, tiled=True)
    blocks = rows_of_all(own_rows.reshape(-1, model_width))
    partials = expert_apply(blocks, expert_weights[0])
    answer = sums_at_owner(partials).reshape(mp_count, capacity, model_width)
    returned = lax.all_to_all(answer, "mp", split_axis=0, concat_axis=0, tiled=True)
    expert_mix = jnp.dot(
        combine_matrix,
        returned.reshape(-1, model_width).astype(jnp.float32),
        precision=lax.Precision.HIGHEST,
    ).astype(jnp.bfloat16)
    return (hidden, expert_mix, placed)


def solution(mesh):
    placed = (
        P("dp", "mp"),
        P("mp", "dp"),
        P(("dp", "mp"), None),
        P(),
        P(),
        P("mp", None, "dp", None),
        P(),
        P(("dp", "mp"), None),
    )
    return jax.shard_map(
        handoff,
        mesh=mesh,
        in_specs=placed,
        out_specs=(P(("dp", "mp"), None), P(("dp", "mp"), None), P(None, None, ("dp", "mp"), None)),
        check_vma=False,
    )
```

profile of v0, /device:TPU:1, one launch (start us, length us, event | category | flops | bytes accessed | tf_op | source)
XLA Modules:
  0.0 208.4 jit_solution(7354183344893586631)
XLA Ops:
  0.7 1.7 broadcast_in_dim.48
  2.4 8.3 %all-to-all-start = ((bf16[8,64,512]{2,1,0:T(8,128)(2,1)}), bf16[8,64,512]{2,1,0:T(8,128)(2,1)S(1)}, u32[]{:S(2)}, u32[]{:S(2)}) async-start(bf16[8,64,512]{2,1,0:T(8,128)(2,1)} %broadcast_in_dim.48), calls=%async_computation | async-start | bytes 1048576 | tf_op jit(solution)/shard_map/all_to_all | solution.py:276
  10.7 1.3 shard_map.103
  12.0 0.8 copy.11
  12.8 0.7 select_reduce_fusion.5
  13.9 7.0 %all-to-all-done = bf16[8,64,512]{2,1,0:T(8,128)(2,1)S(1)} async-done(((bf16[8,64,512]{2,1,0:T(8,128)(2,1)}), bf16[8,64,512]{2,1,0:T(8,128)(2,1)S(1)}, u32[]{:S(2)}, u32[]{:S(2)}) %all-to-all-start) | async-done | bytes 524320 | tf_op jit(solution)/shard_map/all_to_all | solution.py:276
  20.9 0.6 convolution_convert_fusion.2
  21.5 1.0 reshape.153
  22.5 7.3 %all-to-all-start.1 = ((bf16[128,4,640]{2,1,0:T(4,128)(2,1)}), bf16[128,4,640]{2,1,0:T(4,128)(2,1)S(1)}, u32[]{:S(2)}, u32[]{:S(2)}) async-start(bf16[128,4,640]{2,1,0:T(4,128)(2,1)} %reshape.153), calls=%async_computation.1 | async-start | bytes 1310720 | tf_op jit(solution)/shard_map/all_to_all | solution.py:283
  30.4 14.4 %all-to-all-done.1 = bf16[128,4,640]{2,1,0:T(4,128)(2,1)S(1)} async-done(((bf16[128,4,640]{2,1,0:T(4,128)(2,1)}), bf16[128,4,640]{2,1,0:T(4,128)(2,1)S(1)}, u32[]{:S(2)}, u32[]{:S(2)}) %all-to-all-start.1) | async-done | bytes 655392 | tf_op jit(solution)/shard_map/all_to_all | solution.py:283
  45.6 0.8 reshape.156
  46.4 4.3 %all-to-all-start.2 = ((bf16[16,2,5120]{2,1,0:T(2,128)(2,1)}), bf16[16,2,5120]{2,1,0:T(2,128)(2,1)S(1)}, u32[]{:S(2)}, u32[]{:S(2)}) async-start(bf16[16,2,5120]{2,1,0:T(2,128)(2,1)} %reshape.156), calls=%async_computation.2 | async-start | bytes 655360 | tf_op jit(solution)/shard_map/all_to_all | solution.py:318
  50.7 7.7 %all-to-all-done.2 = bf16[16,2,5120]{2,1,0:T(2,128)(2,1)S(1)} async-done(((bf16[16,2,5120]{2,1,0:T(2,128)(2,1)}), bf16[16,2,5120]{2,1,0:T(2,128)(2,1)S(1)}, u32[]{:S(2)}, u32[]{:S(2)}) %all-to-all-start.2) | async-done | bytes 327712 | tf_op jit(solution)/shard_map/all_to_all | solution.py:318
  58.6 0.5 collective-permute-start.3
  59.1 5.1 %dynamic-slice_bitcast_fusion = (bf16[3,24,5120]{2,1,0:T(8,128)(2,1)}, bf16[3,24,5120]{2,1,0:T(8,128)(2,1)}, bf16[3,24,5120]{2,1,0:T(8,128)(2,1)}, bf16[3,24,512...) fusion(bf16[1,3,192,5120]{3,2,1,0:T(8,128)(2,1)} %param.13, ...), kind=kLoop, calls=%fused_computation.10 | loop fusion | bytes 11796512 | tf_op jit(solution)/shard_map/dynamic_slice | solution.py:120
  64.2 1.2 collective-permute-start.17
  65.4 0.5 shard_map.104
  68.3 1.2 shard_map.105
  70.0 2.3 %collective-permute-start.1 = (bf16[32,5120]{1,0:T(8,128)(2,1)S(1)}, bf16[32,5120]{1,0:T(8,128)(2,1)S(1)}, u32[]{:S(2)}, u32[]{:S(2)}) collective-permute-start(bf16[32,5120]{1,0:T(8,128)(2,1)S(1)} %reshape.157.refs_0_), channel_id=1, source_target_pairs={{0,96},{16,112},{32,0},{48,16},{64,32},{80,48},{96,64},{112,80},{1... | collective-permute-start | bytes 983048 | tf_op jit(solution)/shard_map/ppermute | solution.py:233
  72.3 0.6 collective-permute-start.4
  72.9 0.8 select_reduce_fusion.4
  73.7 6.8 %collective-permute-done.refs_1_ = bf16[32,5120]{1,0:T(8,128)(2,1)S(1)} collective-permute-done((bf16[32,5120]{1,0:T(8,128)(2,1)S(1)}, bf16[32,5120]{1,0:T(8,128)(2,1)S(1)}, u32[]{:S(2)}, u32[]{:S(2)}) %collective-permute-start) | collective-permute-done | bytes 327712 | tf_op jit(solution)/shard_map/ppermute | solution.py:233
  80.8 6.9 %collective-permute-start.19 = (bf16[3,24,5120]{2,1,0:T(8,128)(2,1)}, bf16[3,24,5120]{2,1,0:T(8,128)(2,1)}, u32[]{:S(2)}, u32[]{:S(2)}) collective-permute-start(bf16[3,24,5120]{2,1,0:T(8,128)(2,1)} %get-tuple-element.31), channel_id=1, source_target_pairs={{0,14},{1,15},{2,8},{3,9},{4,10},{5,11},{6,12},{7,13},{8,6},{9,7},... | collective-permute-start | bytes 2211848 | tf_op jit(solution)/shard_map/ppermute | solution.py:136
  87.7 3.2 %collective-permute-start.5 = (bf16[32,5120]{1,0:T(8,128)(2,1)S(1)}, bf16[32,5120]{1,0:T(8,128)(2,1)S(1)}, u32[]{:S(2)}, u32[]{:S(2)}) collective-permute-start(bf16[32,5120]{1,0:T(8,128)(2,1)S(1)} %collective-permute-done.3.refs_4_), channel_id=1, source_target_pairs={{0,96},{16,112},{32,0},{48,16},{64,32},{80,48},{96,64},{112,80},{1... | collective-permute-start | bytes 983048 | tf_op jit(solution)/shard_map/ppermute | solution.py:233
  90.9 3.0 %collective-permute-done.4.refs_5_ = bf16[32,5120]{1,0:T(8,128)(2,1)S(1)} collective-permute-done((bf16[32,5120]{1,0:T(8,128)(2,1)S(1)}, bf16[32,5120]{1,0:T(8,128)(2,1)S(1)}, u32[]{:S(2)}, u32[]{:S(2)}) %collective-permute-start.4) | collective-permute-done | bytes 327712 | tf_op jit(solution)/shard_map/ppermute | solution.py:233
  93.9 0.7 copy-done.11
  94.7 3.6 %collective-permute-done.5.refs_6_ = bf16[32,5120]{1,0:T(8,128)(2,1)S(1)} collective-permute-done((bf16[32,5120]{1,0:T(8,128)(2,1)S(1)}, bf16[32,5120]{1,0:T(8,128)(2,1)S(1)}, u32[]{:S(2)}, u32[]{:S(2)}) %collective-permute-start.5) | collective-permute-done | bytes 327712 | tf_op jit(solution)/shard_map/ppermute | solution.py:233
  98.3 5.3 %collective-permute-done.6.refs_7_ = bf16[32,5120]{1,0:T(8,128)(2,1)S(1)} collective-permute-done((bf16[32,5120]{1,0:T(8,128)(2,1)S(1)}, bf16[32,5120]{1,0:T(8,128)(2,1)S(1)}, u32[]{:S(2)}, u32[]{:S(2)}) %collective-permute-start.6) | collective-permute-done | bytes 327712 | tf_op jit(solution)/shard_map/ppermute | solution.py:233
  103.8 2.7 %copy-done.1 = bf16[1,3,192,5120]{3,2,1,0:T(8,128)(2,1)S(1)} copy-done((bf16[1,3,192,5120]{3,2,1,0:T(8,128)(2,1)S(1)}, bf16[1,3,192,5120]{3,2,1,0:T(8,128)(2,1)}, u32[]{:S(2)}) %copy-start.1) | copy-done | bytes 5898264
  106.5 1.0 copy-done.12
  107.5 7.9 %experts.1 = (bf16[32,5120]{1,0:T(8,128)(2,1)S(1)}, bf16[32,5120]{1,0:T(8,128)(2,1)S(1)}, bf16[32,5120]{1,0:T(8,128)(2,1)S(1)}, bf16[32,5120]{1,0:T(8,128)(2,1)S...) custom-call(bf16[32,5120]{1,0:T(8,128)(2,1)S(1)} %reshape.157.refs_0, ...), custom_call_target="tpu_custom_call" | custom-call | flops 4294967296 | bytes 12582912 | tf_op jit(solution)/shard_map/experts/pallas_call | solution.py:201
  115.4 0.7 copy-done.10
  116.1 0.7 copy-done.13
  116.9 0.7 copy-done.14
  117.6 0.7 copy-done.15
  118.3 1.5 collective-permute-start.7
  119.8 1.8 collective-permute-start.9
  121.6 1.1 and_convert_fusion
  122.7 1.8 reshape.161.chooser
  124.5 1.2 fusion.2
  125.7 4.5 %collective-permute-start.15 = (bf16[3,24,5120]{2,1,0:T(8,128)(2,1)}, bf16[3,24,5120]{2,1,0:T(8,128)(2,1)S(1)}, u32[]{:S(2)}, u32[]{:S(2)}) collective-permute-start(bf16[3,24,5120]{2,1,0:T(8,128)(2,1)} %get-tuple-element.27), channel_id=1, source_target_pairs={{0,6},{1,7},{2,0},{3,1},{4,2},{5,3},{6,4},{7,5},{8,14},{9,15},{10,... | collective-permute-start | bytes 2211848 | tf_op jit(solution)/shard_map/ppermute | solution.py:136
  130.2 11.2 %collective-permute-done.14.refs_1_ = bf16[3,24,5120]{2,1,0:T(8,128)(2,1)} collective-permute-done((bf16[3,24,5120]{2,1,0:T(8,128)(2,1)}, bf16[3,24,5120]{2,1,0:T(8,128)(2,1)}, u32[]{:S(2)}, u32[]{:S(2)}) %collective-permute-start.14) | collective-permute-done | bytes 737312 | tf_op jit(solution)/shard_map/ppermute | solution.py:136
  141.4 1.8 collective-permute-start.16
  143.2 4.4 %collective-permute-start.21 = (bf16[3,24,5120]{2,1,0:T(8,128)(2,1)S(1)}, bf16[3,24,5120]{2,1,0:T(8,128)(2,1)S(1)}, u32[]{:S(2)}, u32[]{:S(2)}) collective-permute-start(bf16[3,24,5120]{2,1,0:T(8,128)(2,1)S(1)} %get-tuple-element.43.refs_0_), channel_id=1, source_target_pairs={{0,1},{1,0},{2,3},{3,2},{4,5},{5,4},{6,7},{7,6},{8,9},{9,8},{10,11... | collective-permute-start | bytes 2211848 | tf_op jit(solution)/shard_map/ppermute | solution.py:140
  147.7 0.4 collective-permute-start.26
  148.1 2.1 %add_convert_fusion.1 = bf16[32,5120]{1,0:T(8,128)(2,1)} fusion(bf16[32,5120]{1,0:T(8,128)(2,1)} %collective-permute-done.9, bf16[32,5120]{1,0:T(8,128)(2,1)} %collective-permute-done.8, bf16[32,5120]{1,0:T(8,128)(2,1)} %collective-permute-done.7, bf16[32,5120]{1,0:T(8,128)(2,1)S(1)} %get-tuple-element.18), kind=kLoop, calls=%fused_computation.19 | loop fusion | flops 1310720 | bytes 1638400 | tf_op jit(solution)/shard_map/convert_element_type | solution.py:241
  150.2 8.1 %collective-permute-start.11 = (bf16[32,5120]{1,0:T(8,128)(2,1)}, bf16[32,5120]{1,0:T(8,128)(2,1)S(1)}, u32[]{:S(2)}, u32[]{:S(2)}) collective-permute-start(bf16[32,5120]{1,0:T(8,128)(2,1)} %copy-done.15), channel_id=1, source_target_pairs={{0,96},{16,112},{32,0},{48,16},{64,32},{80,48},{96,64},{112,80},{1... | collective-permute-start | bytes 983048 | tf_op jit(solution)/shard_map/ppermute | solution.py:251
  158.4 3.6 %collective-permute-start.12 = (bf16[32,5120]{1,0:T(8,128)(2,1)}, bf16[32,5120]{1,0:T(8,128)(2,1)}, u32[]{:S(2)}, u32[]{:S(2)}) collective-permute-start(bf16[32,5120]{1,0:T(8,128)(2,1)} %copy-done.14), channel_id=1, source_target_pairs={{0,32},{16,48},{32,64},{48,80},{64,96},{80,112},{96,0},{112,16},{1... | collective-permute-start | bytes 983048 | tf_op jit(solution)/shard_map/ppermute | solution.py:251
  161.9 0.9 copy-done.6
  162.8 0.9 copy-done.8
  163.8 3.2 %collective-permute-start.10 = (bf16[32,5120]{1,0:T(8,128)(2,1)}, bf16[32,5120]{1,0:T(8,128)(2,1)}, u32[]{:S(2)}, u32[]{:S(2)}) collective-permute-start(bf16[32,5120]{1,0:T(8,128)(2,1)} %add_convert_fusion.1), channel_id=1, source_target_pairs={{0,16},{16,0},{32,48},{48,32},{64,80},{80,64},{96,112},{112,96},{1... | collective-permute-start | bytes 983048 | tf_op jit(solution)/shard_map/ppermute | solution.py:253
  167.4 4.4 %collective-permute-start.27 = (bf16[3,24,5120]{2,1,0:T(8,128)(2,1)}, bf16[3,24,5120]{2,1,0:T(8,128)(2,1)}, u32[]{:S(2)}, u32[]{:S(2)}) collective-permute-start(bf16[3,24,5120]{2,1,0:T(8,128)(2,1)} %collective-permute-done.19.refs_6_), channel_id=1, source_target_pairs={{0,1},{1,0},{2,3},{3,2},{4,5},{5,4},{6,7},{7,6},{8,9},{9,8},{10,11... | collective-permute-start | bytes 2211848 | tf_op jit(solution)/shard_map/ppermute | solution.py:140
  171.8 2.2 %collective-permute-start.28 = (bf16[3,24,5120]{2,1,0:T(8,128)(2,1)}, bf16[3,24,5120]{2,1,0:T(8,128)(2,1)}, u32[]{:S(2)}, u32[]{:S(2)}) collective-permute-start(bf16[3,24,5120]{2,1,0:T(8,128)(2,1)} %collective-permute-done.20.refs_7_), channel_id=1, source_target_pairs={{0,1},{1,0},{2,3},{3,2},{4,5},{5,4},{6,7},{7,6},{8,9},{9,8},{10,11... | collective-permute-start | bytes 2211848 | tf_op jit(solution)/shard_map/ppermute | solution.py:140
  174.1 0.5 collective-permute-done.13
  174.6 3.5 %collective-permute-start.23 = (bf16[3,24,5120]{2,1,0:T(8,128)(2,1)}, bf16[3,24,5120]{2,1,0:T(8,128)(2,1)}, u32[]{:S(2)}, u32[]{:S(2)}) collective-permute-start(bf16[3,24,5120]{2,1,0:T(8,128)(2,1)} %copy-done.2), channel_id=1, source_target_pairs={{0,1},{1,0},{2,3},{3,2},{4,5},{5,4},{6,7},{7,6},{8,9},{9,8},{10,11... | collective-permute-start | bytes 2211848 | tf_op jit(solution)/shard_map/ppermute | solution.py:140
  178.1 1.6 add_convert_fusion
  179.7 0.8 reshape.158
  180.5 11.3 %all-to-all-start.3 = ((bf16[16,2,5120]{2,1,0:T(2,128)(2,1)}), bf16[16,2,5120]{2,1,0:T(2,128)(2,1)S(1)}, u32[]{:S(2)}, u32[]{:S(2)}) async-start(bf16[16,2,5120]{2,1,0:T(2,128)(2,1)} %reshape.158), calls=%async_computation.3 | async-start | bytes 655360 | tf_op jit(solution)/shard_map/all_to_all | solution.py:322
  192.1 1.1 copy-done.3
  193.2 1.1 copy-done.5
  194.3 1.1 copy-done.7
  195.4 1.1 copy-done.9
  196.5 10.9 %placing.1 = bf16[3,12,16,5120]{3,2,1,0:T(8,128)(2,1)} custom-call(s32[1]{0:T(128)} %bitcast.6.meta, bf16[192,256]{1,0:T(8,128)(2,1)S(1)} %reshape.161.chooser, bf16[3,24,5120]{2,1,0:T(8,128)(2,1)S(1)} %get-tuple-element.43.refs_0_, bf16[3,24,5120]{2,1,0:T(8,128)(2,1)} %collective-permute-done.14.refs_1_, bf16[3,24,5120]{2,1,0:T(8,128)(2,1)S(1)} %copy-done.3, ...), custom_call_target="tpu_custom_call" | custom-call | flops 2147483648 | bytes 16777216 | tf_op jit(solution)/shard_map/placing/pallas_call | solution.py:82
  207.6 0.9 convolution_convert_fusion.1
  (89 shorter events, 4.0 us)
Async XLA Ops:
  0.6 20.3 %copy-start = (bf16[512,640]{1,0:T(8,128)(2,1)S(1)}, bf16[512,640]{1,0:T(8,128)(2,1)}, u32[]{:S(2)}) copy-start(bf16[512,640]{1,0:T(8,128)(2,1)} %param.9) | copy-start | bytes 1966084
  0.6 44.4 %copy-start.18 = (bf16[4,5120]{1,0:T(4,128)(2,1)S(1)}, bf16[4,5120]{1,0:T(4,128)(2,1)}, u32[]{:S(2)}) copy-start(bf16[4,5120]{1,0:T(4,128)(2,1)} %param.10) | copy-start | bytes 122884
  0.7 44.6 %copy-start.19 = (f32[5120]{0:T(1024)S(1)}, f32[5120]{0:T(1024)}, u32[]{:S(2)}) copy-start(f32[5120]{0:T(1024)} %param.11) | copy-start | bytes 61444
  2.4 18.5 %all-to-all-start = ((bf16[8,64,512]{2,1,0:T(8,128)(2,1)}), bf16[8,64,512]{2,1,0:T(8,128)(2,1)S(1)}, u32[]{:S(2)}, u32[]{:S(2)}) async-start(bf16[8,64,512]{2,1,0:T(8,128)(2,1)} %broadcast_in_dim.48), calls=%async_computation | async-start | bytes 1048576 | tf_op jit(solution)/shard_map/all_to_all | solution.py:276
  22.5 22.3 %all-to-all-start.1 = ((bf16[128,4,640]{2,1,0:T(4,128)(2,1)}), bf16[128,4,640]{2,1,0:T(4,128)(2,1)S(1)}, u32[]{:S(2)}, u32[]{:S(2)}) async-start(bf16[128,4,640]{2,1,0:T(4,128)(2,1)} %reshape.153), calls=%async_computation.1 | async-start | bytes 1310720 | tf_op jit(solution)/shard_map/all_to_all | solution.py:283
  30.1 15.1 %copy-start.20 = (s32[24]{0:T(128)}, s32[24]{0:T(128)S(1)}, u32[]{:S(2)}) copy-start(s32[24]{0:T(128)S(1)} %get-tuple-element.46) | copy-start | bytes 292
  45.2 13.4 %copy-start.17 = (bf16[4,5120]{1,0:T(4,128)(2,1)}, bf16[4,5120]{1,0:T(4,128)(2,1)S(1)}, u32[]{:S(2)}) copy-start(bf16[4,5120]{1,0:T(4,128)(2,1)S(1)} %get-tuple-element.36) | copy-start | bytes 122884
  46.4 12.0 %all-to-all-start.2 = ((bf16[16,2,5120]{2,1,0:T(2,128)(2,1)}), bf16[16,2,5120]{2,1,0:T(2,128)(2,1)S(1)}, u32[]{:S(2)}, u32[]{:S(2)}) async-start(bf16[16,2,5120]{2,1,0:T(2,128)(2,1)} %reshape.156), calls=%async_computation.2 | async-start | bytes 655360 | tf_op jit(solution)/shard_map/all_to_all | solution.py:318
  58.6 13.7 %collective-permute-start.3 = (bf16[32,5120]{1,0:T(8,128)(2,1)S(1)}, bf16[32,5120]{1,0:T(8,128)(2,1)S(1)}, u32[]{:S(2)}, u32[]{:S(2)}) collective-permute-start(bf16[32,5120]{1,0:T(8,128)(2,1)S(1)} %reshape.157.refs_0_), channel_id=1, source_target_pairs={{0,16},{16,0},{32,48},{48,32},{64,80},{80,64},{96,112},{112,96},{1... | collective-permute-start | bytes 983048 | tf_op jit(solution)/shard_map/ppermute | solution.py:228
  64.2 54.1 %collective-permute-start.17 = (bf16[3,24,5120]{2,1,0:T(8,128)(2,1)}, bf16[3,24,5120]{2,1,0:T(8,128)(2,1)S(1)}, u32[]{:S(2)}, u32[]{:S(2)}) collective-permute-start(bf16[3,24,5120]{2,1,0:T(8,128)(2,1)} %get-tuple-element.29), channel_id=1, source_target_pairs={{0,4},{1,5},{2,6},{3,7},{4,0},{5,1},{6,2},{7,3},{8,12},{9,13},{10,... | collective-permute-start | bytes 2211848 | tf_op jit(solution)/shard_map/ppermute | solution.py:136
  69.6 11.0 %collective-permute-start = (bf16[32,5120]{1,0:T(8,128)(2,1)S(1)}, bf16[32,5120]{1,0:T(8,128)(2,1)S(1)}, u32[]{:S(2)}, u32[]{:S(2)}) collective-permute-start(bf16[32,5120]{1,0:T(8,128)(2,1)S(1)} %reshape.157.refs_0_), channel_id=1, source_target_pairs={{0,32},{16,48},{32,64},{48,80},{64,96},{80,112},{96,0},{112,16},{1... | collective-permute-start | bytes 983048 | tf_op jit(solution)/shard_map/ppermute | solution.py:233
  70.0 10.8 %collective-permute-start.1 = (bf16[32,5120]{1,0:T(8,128)(2,1)S(1)}, bf16[32,5120]{1,0:T(8,128)(2,1)S(1)}, u32[]{:S(2)}, u32[]{:S(2)}) collective-permute-start(bf16[32,5120]{1,0:T(8,128)(2,1)S(1)} %reshape.157.refs_0_), channel_id=1, source_target_pairs={{0,96},{16,112},{32,0},{48,16},{64,32},{80,48},{96,64},{112,80},{1... | collective-permute-start | bytes 983048 | tf_op jit(solution)/shard_map/ppermute | solution.py:233
  72.3 15.4 %collective-permute-start.2 = (bf16[32,5120]{1,0:T(8,128)(2,1)S(1)}, bf16[32,5120]{1,0:T(8,128)(2,1)S(1)}, u32[]{:S(2)}, u32[]{:S(2)}) collective-permute-start(bf16[32,5120]{1,0:T(8,128)(2,1)S(1)} %reshape.157.refs_0_), channel_id=1, source_target_pairs={{0,64},{16,80},{32,96},{48,112},{64,0},{80,16},{96,32},{112,48},{1... | collective-permute-start | bytes 983048 | tf_op jit(solution)/shard_map/ppermute | solution.py:233
  72.3 21.6 %collective-permute-start.4 = (bf16[32,5120]{1,0:T(8,128)(2,1)S(1)}, bf16[32,5120]{1,0:T(8,128)(2,1)S(1)}, u32[]{:S(2)}, u32[]{:S(2)}) collective-permute-start(bf16[32,5120]{1,0:T(8,128)(2,1)S(1)} %collective-permute-done.3.refs_4_), channel_id=1, source_target_pairs={{0,32},{16,48},{32,64},{48,80},{64,96},{80,112},{96,0},{112,16},{1... | collective-permute-start | bytes 983048 | tf_op jit(solution)/shard_map/ppermute | solution.py:233
  80.5 39.3 %collective-permute-start.18 = (bf16[3,24,5120]{2,1,0:T(8,128)(2,1)}, bf16[3,24,5120]{2,1,0:T(8,128)(2,1)S(1)}, u32[]{:S(2)}, u32[]{:S(2)}) collective-permute-start(bf16[3,24,5120]{2,1,0:T(8,128)(2,1)} %get-tuple-element.30), channel_id=1, source_target_pairs={{0,10},{1,11},{2,12},{3,13},{4,14},{5,15},{6,8},{7,9},{8,2},{9,3},... | collective-permute-start | bytes 2211848 | tf_op jit(solution)/shard_map/ppermute | solution.py:136
  80.8 39.0 %collective-permute-start.19 = (bf16[3,24,5120]{2,1,0:T(8,128)(2,1)}, bf16[3,24,5120]{2,1,0:T(8,128)(2,1)}, u32[]{:S(2)}, u32[]{:S(2)}) collective-permute-start(bf16[3,24,5120]{2,1,0:T(8,128)(2,1)} %get-tuple-element.31), channel_id=1, source_target_pairs={{0,14},{1,15},{2,8},{3,9},{4,10},{5,11},{6,12},{7,13},{8,6},{9,7},... | collective-permute-start | bytes 2211848 | tf_op jit(solution)/shard_map/ppermute | solution.py:136
  87.7 10.6 %collective-permute-start.5 = (bf16[32,5120]{1,0:T(8,128)(2,1)S(1)}, bf16[32,5120]{1,0:T(8,128)(2,1)S(1)}, u32[]{:S(2)}, u32[]{:S(2)}) collective-permute-start(bf16[32,5120]{1,0:T(8,128)(2,1)S(1)} %collective-permute-done.3.refs_4_), channel_id=1, source_target_pairs={{0,96},{16,112},{32,0},{48,16},{64,32},{80,48},{96,64},{112,80},{1... | collective-permute-start | bytes 983048 | tf_op jit(solution)/shard_map/ppermute | solution.py:233
  93.9 9.7 %collective-permute-start.6 = (bf16[32,5120]{1,0:T(8,128)(2,1)S(1)}, bf16[32,5120]{1,0:T(8,128)(2,1)S(1)}, u32[]{:S(2)}, u32[]{:S(2)}) collective-permute-start(bf16[32,5120]{1,0:T(8,128)(2,1)S(1)} %collective-permute-done.3.refs_4_), channel_id=1, source_target_pairs={{0,64},{16,80},{32,96},{48,112},{64,0},{80,16},{96,32},{112,48},{1... | collective-permute-start | bytes 983048 | tf_op jit(solution)/shard_map/ppermute | solution.py:233
  93.9 0.7 copy-start.11
  98.3 27.4 %collective-permute-start.20 = (bf16[3,24,5120]{2,1,0:T(8,128)(2,1)}, bf16[3,24,5120]{2,1,0:T(8,128)(2,1)}, u32[]{:S(2)}, u32[]{:S(2)}) collective-permute-start(bf16[3,24,5120]{2,1,0:T(8,128)(2,1)} %get-tuple-element.32), channel_id=1, source_target_pairs={{0,12},{1,13},{2,14},{3,15},{4,8},{5,9},{6,10},{7,11},{8,4},{9,5},... | collective-permute-start | bytes 2211848 | tf_op jit(solution)/shard_map/ppermute | solution.py:136
  103.6 37.8 %collective-permute-start.14 = (bf16[3,24,5120]{2,1,0:T(8,128)(2,1)}, bf16[3,24,5120]{2,1,0:T(8,128)(2,1)}, u32[]{:S(2)}, u32[]{:S(2)}) collective-permute-start(bf16[3,24,5120]{2,1,0:T(8,128)(2,1)} %get-tuple-element.26), channel_id=1, source_target_pairs={{0,2},{1,3},{2,4},{3,5},{4,6},{5,7},{6,0},{7,1},{8,10},{9,11},{10,... | collective-permute-start | bytes 2211848 | tf_op jit(solution)/shard_map/ppermute | solution.py:136
  103.8 2.7 %copy-start.1 = (bf16[1,3,192,5120]{3,2,1,0:T(8,128)(2,1)S(1)}, bf16[1,3,192,5120]{3,2,1,0:T(8,128)(2,1)}, u32[]{:S(2)}) copy-start(bf16[1,3,192,5120]{3,2,1,0:T(8,128)(2,1)} %param.13) | copy-start | bytes 17694724
  106.5 1.0 copy-start.12
  115.4 0.7 copy-start.10
  116.1 0.7 copy-start.13
  116.9 0.7 copy-start.14
  117.6 0.7 copy-start.15
  118.3 73.5 %copy-start.21 = (s32[24]{0:T(128)S(1)}, s32[24]{0:T(128)}, u32[]{:S(2)}) copy-start(s32[24]{0:T(128)} %copy-done.20) | copy-start | bytes 292
  118.3 24.8 %collective-permute-start.7 = (bf16[32,5120]{1,0:T(8,128)(2,1)}, bf16[32,5120]{1,0:T(8,128)(2,1)}, u32[]{:S(2)}, u32[]{:S(2)}) collective-permute-start(bf16[32,5120]{1,0:T(8,128)(2,1)} %get-tuple-element.19), channel_id=1, source_target_pairs={{0,96},{16,112},{32,0},{48,16},{64,32},{80,48},{96,64},{112,80},{1... | collective-permute-start | bytes 983048 | tf_op jit(solution)/shard_map/ppermute | solution.py:251
  119.8 27.8 %collective-permute-start.8 = (bf16[32,5120]{1,0:T(8,128)(2,1)}, bf16[32,5120]{1,0:T(8,128)(2,1)}, u32[]{:S(2)}, u32[]{:S(2)}) collective-permute-start(bf16[32,5120]{1,0:T(8,128)(2,1)} %get-tuple-element.20), channel_id=1, source_target_pairs={{0,32},{16,48},{32,64},{48,80},{64,96},{80,112},{96,0},{112,16},{1... | collective-permute-start | bytes 983048 | tf_op jit(solution)/shard_map/ppermute | solution.py:251
  119.8 27.9 %collective-permute-start.9 = (bf16[32,5120]{1,0:T(8,128)(2,1)}, bf16[32,5120]{1,0:T(8,128)(2,1)}, u32[]{:S(2)}, u32[]{:S(2)}) collective-permute-start(bf16[32,5120]{1,0:T(8,128)(2,1)} %get-tuple-element.21), channel_id=1, source_target_pairs={{0,64},{16,80},{32,96},{48,112},{64,0},{80,16},{96,32},{112,48},{1... | collective-permute-start | bytes 983048 | tf_op jit(solution)/shard_map/ppermute | solution.py:251
  125.7 24.5 %collective-permute-start.15 = (bf16[3,24,5120]{2,1,0:T(8,128)(2,1)}, bf16[3,24,5120]{2,1,0:T(8,128)(2,1)S(1)}, u32[]{:S(2)}, u32[]{:S(2)}) collective-permute-start(bf16[3,24,5120]{2,1,0:T(8,128)(2,1)} %get-tuple-element.27), channel_id=1, source_target_pairs={{0,6},{1,7},{2,0},{3,1},{4,2},{5,3},{6,4},{7,5},{8,14},{9,15},{10,... | collective-permute-start | bytes 2211848 | tf_op jit(solution)/shard_map/ppermute | solution.py:136
  141.4 17.0 %collective-permute-start.16 = (bf16[3,24,5120]{2,1,0:T(8,128)(2,1)}, bf16[3,24,5120]{2,1,0:T(8,128)(2,1)S(1)}, u32[]{:S(2)}, u32[]{:S(2)}) collective-permute-start(bf16[3,24,5120]{2,1,0:T(8,128)(2,1)} %get-tuple-element.28), channel_id=1, source_target_pairs={{0,8},{1,9},{2,10},{3,11},{4,12},{5,13},{6,14},{7,15},{8,0},{9,1},... | collective-permute-start | bytes 2211848 | tf_op jit(solution)/shard_map/ppermute | solution.py:136
  143.2 18.8 %collective-permute-start.21 = (bf16[3,24,5120]{2,1,0:T(8,128)(2,1)S(1)}, bf16[3,24,5120]{2,1,0:T(8,128)(2,1)S(1)}, u32[]{:S(2)}, u32[]{:S(2)}) collective-permute-start(bf16[3,24,5120]{2,1,0:T(8,128)(2,1)S(1)} %get-tuple-element.43.refs_0_), channel_id=1, source_target_pairs={{0,1},{1,0},{2,3},{3,2},{4,5},{5,4},{6,7},{7,6},{8,9},{9,8},{10,11... | collective-permute-start | bytes 2211848 | tf_op jit(solution)/shard_map/ppermute | solution.py:140
  147.6 15.2 %collective-permute-start.25 = (bf16[3,24,5120]{2,1,0:T(8,128)(2,1)S(1)}, bf16[3,24,5120]{2,1,0:T(8,128)(2,1)S(1)}, u32[]{:S(2)}, u32[]{:S(2)}) collective-permute-start(bf16[3,24,5120]{2,1,0:T(8,128)(2,1)S(1)} %collective-permute-done.17.refs_4_), channel_id=1, source_target_pairs={{0,1},{1,0},{2,3},{3,2},{4,5},{5,4},{6,7},{7,6},{8,9},{9,8},{10,11... | collective-permute-start | bytes 2211848 | tf_op jit(solution)/shard_map/ppermute | solution.py:140
  147.7 19.7 %collective-permute-start.26 = (bf16[3,24,5120]{2,1,0:T(8,128)(2,1)S(1)}, bf16[3,24,5120]{2,1,0:T(8,128)(2,1)}, u32[]{:S(2)}, u32[]{:S(2)}) collective-permute-start(bf16[3,24,5120]{2,1,0:T(8,128)(2,1)S(1)} %collective-permute-done.18.refs_5_), channel_id=1, source_target_pairs={{0,1},{1,0},{2,3},{3,2},{4,5},{5,4},{6,7},{7,6},{8,9},{9,8},{10,11... | collective-permute-start | bytes 2211848 | tf_op jit(solution)/shard_map/ppermute | solution.py:140
  150.2 12.6 %copy-start.2 = (bf16[3,24,5120]{2,1,0:T(8,128)(2,1)}, bf16[3,24,5120]{2,1,0:T(8,128)(2,1)S(1)}, u32[]{:S(2)}) copy-start(bf16[3,24,5120]{2,1,0:T(8,128)(2,1)S(1)} %collective-permute-done.15.refs_2_) | copy-start | bytes 2211844
  150.2 21.6 %collective-permute-start.11 = (bf16[32,5120]{1,0:T(8,128)(2,1)}, bf16[32,5120]{1,0:T(8,128)(2,1)S(1)}, u32[]{:S(2)}, u32[]{:S(2)}) collective-permute-start(bf16[32,5120]{1,0:T(8,128)(2,1)} %copy-done.15), channel_id=1, source_target_pairs={{0,96},{16,112},{32,0},{48,16},{64,32},{80,48},{96,64},{112,80},{1... | collective-permute-start | bytes 983048 | tf_op jit(solution)/shard_map/ppermute | solution.py:251
  158.4 8.6 %copy-start.4 = (bf16[3,24,5120]{2,1,0:T(8,128)(2,1)}, bf16[3,24,5120]{2,1,0:T(8,128)(2,1)S(1)}, u32[]{:S(2)}) copy-start(bf16[3,24,5120]{2,1,0:T(8,128)(2,1)S(1)} %collective-permute-done.16.refs_3_) | copy-start | bytes 2211844
  158.4 15.7 %collective-permute-start.12 = (bf16[32,5120]{1,0:T(8,128)(2,1)}, bf16[32,5120]{1,0:T(8,128)(2,1)}, u32[]{:S(2)}, u32[]{:S(2)}) collective-permute-start(bf16[32,5120]{1,0:T(8,128)(2,1)} %copy-done.14), channel_id=1, source_target_pairs={{0,32},{16,48},{32,64},{48,80},{64,96},{80,112},{96,0},{112,16},{1... | collective-permute-start | bytes 983048 | tf_op jit(solution)/shard_map/ppermute | solution.py:251
  161.9 0.9 copy-start.6
  162.8 11.8 %collective-permute-start.13 = (bf16[32,5120]{1,0:T(8,128)(2,1)}, bf16[32,5120]{1,0:T(8,128)(2,1)}, u32[]{:S(2)}, u32[]{:S(2)}) collective-permute-start(bf16[32,5120]{1,0:T(8,128)(2,1)} %copy-done.13), channel_id=1, source_target_pairs={{0,64},{16,80},{32,96},{48,112},{64,0},{80,16},{96,32},{112,48},{1... | collective-permute-start | bytes 983048 | tf_op jit(solution)/shard_map/ppermute | solution.py:251
  162.8 0.9 copy-start.8
  163.8 14.3 %collective-permute-start.10 = (bf16[32,5120]{1,0:T(8,128)(2,1)}, bf16[32,5120]{1,0:T(8,128)(2,1)}, u32[]{:S(2)}, u32[]{:S(2)}) collective-permute-start(bf16[32,5120]{1,0:T(8,128)(2,1)} %add_convert_fusion.1), channel_id=1, source_target_pairs={{0,16},{16,0},{32,48},{48,32},{64,80},{80,64},{96,112},{112,96},{1... | collective-permute-start | bytes 983048 | tf_op jit(solution)/shard_map/ppermute | solution.py:253
  167.4 24.6 %collective-permute-start.27 = (bf16[3,24,5120]{2,1,0:T(8,128)(2,1)}, bf16[3,24,5120]{2,1,0:T(8,128)(2,1)}, u32[]{:S(2)}, u32[]{:S(2)}) collective-permute-start(bf16[3,24,5120]{2,1,0:T(8,128)(2,1)} %collective-permute-done.19.refs_6_), channel_id=1, source_target_pairs={{0,1},{1,0},{2,3},{3,2},{4,5},{5,4},{6,7},{7,6},{8,9},{9,8},{10,11... | collective-permute-start | bytes 2211848 | tf_op jit(solution)/shard_map/ppermute | solution.py:140
  171.8 6.3 %copy-start.16 = (bf16[32,5120]{1,0:T(8,128)(2,1)}, bf16[32,5120]{1,0:T(8,128)(2,1)S(1)}, u32[]{:S(2)}) copy-start(bf16[32,5120]{1,0:T(8,128)(2,1)S(1)} %collective-permute-done.11) | copy-start | bytes 983044
  171.8 20.2 %collective-permute-start.28 = (bf16[3,24,5120]{2,1,0:T(8,128)(2,1)}, bf16[3,24,5120]{2,1,0:T(8,128)(2,1)}, u32[]{:S(2)}, u32[]{:S(2)}) collective-permute-start(bf16[3,24,5120]{2,1,0:T(8,128)(2,1)} %collective-permute-done.20.refs_7_), channel_id=1, source_target_pairs={{0,1},{1,0},{2,3},{3,2},{4,5},{5,4},{6,7},{7,6},{8,9},{9,8},{10,11... | collective-permute-start | bytes 2211848 | tf_op jit(solution)/shard_map/ppermute | solution.py:140
  174.1 18.0 %collective-permute-start.22 = (bf16[3,24,5120]{2,1,0:T(8,128)(2,1)}, bf16[3,24,5120]{2,1,0:T(8,128)(2,1)}, u32[]{:S(2)}, u32[]{:S(2)}) collective-permute-start(bf16[3,24,5120]{2,1,0:T(8,128)(2,1)} %collective-permute-done.14.refs_1_), channel_id=1, source_target_pairs={{0,1},{1,0},{2,3},{3,2},{4,5},{5,4},{6,7},{7,6},{8,9},{9,8},{10,11... | collective-permute-start | bytes 2211848 | tf_op jit(solution)/shard_map/ppermute | solution.py:140
  174.6 17.4 %collective-permute-start.23 = (bf16[3,24,5120]{2,1,0:T(8,128)(2,1)}, bf16[3,24,5120]{2,1,0:T(8,128)(2,1)}, u32[]{:S(2)}, u32[]{:S(2)}) collective-permute-start(bf16[3,24,5120]{2,1,0:T(8,128)(2,1)} %copy-done.2), channel_id=1, source_target_pairs={{0,1},{1,0},{2,3},{3,2},{4,5},{5,4},{6,7},{7,6},{8,9},{9,8},{10,11... | collective-permute-start | bytes 2211848 | tf_op jit(solution)/shard_map/ppermute | solution.py:140
  178.1 14.0 %collective-permute-start.24 = (bf16[3,24,5120]{2,1,0:T(8,128)(2,1)}, bf16[3,24,5120]{2,1,0:T(8,128)(2,1)}, u32[]{:S(2)}, u32[]{:S(2)}) collective-permute-start(bf16[3,24,5120]{2,1,0:T(8,128)(2,1)} %copy-done.4), channel_id=1, source_target_pairs={{0,1},{1,0},{2,3},{3,2},{4,5},{5,4},{6,7},{7,6},{8,9},{9,8},{10,11... | collective-permute-start | bytes 2211848 | tf_op jit(solution)/shard_map/ppermute | solution.py:140
  180.5 26.9 %all-to-all-start.3 = ((bf16[16,2,5120]{2,1,0:T(2,128)(2,1)}), bf16[16,2,5120]{2,1,0:T(2,128)(2,1)S(1)}, u32[]{:S(2)}, u32[]{:S(2)}) async-start(bf16[16,2,5120]{2,1,0:T(2,128)(2,1)} %reshape.158), calls=%async_computation.3 | async-start | bytes 655360 | tf_op jit(solution)/shard_map/all_to_all | solution.py:322
  192.1 1.1 copy-start.3
  193.2 1.1 copy-start.5
  194.3 1.1 copy-start.7
  195.4 1.1 copy-start.9
where the time goes:
time: 209 us; the launch traced here: 208 us
  starting transfers between devices  86.4 us (41%)
  waiting for transfers between devices  59.6 us (29%)
  local copies, waits for them, and re-layouts  26.3 us (13%)
  Pallas kernels  21.8 us (10%)
  other arithmetic  7.61 us (4%)
  matrix products  3.4 us (2%)
  between operations  3.28 us (2%)
    ppermute x6, waiting for transfers between devices, rows_of_all(): groups[-1].append(lax.ppermute(block, 'dp', row_pairs(dy, 0)))  18.7 us
    ppermute x8, starting transfers between devices, moved_experts(): swapped.append(lax.ppermute(block, 'mp', CORE_PAIRS))  15.1 us
    ppermute x6, starting transfers between devices, sums_at_owner(): came.append(lax.ppermute(block, 'dp', row_pairs(-dy, 0)))  15 us
    ppermute x7, starting transfers between devices, moved_experts(): blocks.append(lax.ppermute(block, 'mp', chip_pairs(*shift)))  14.9 us
    all_to_all x1, waiting for transfers between devices, handoff(): summed = lax.all_to_all(partial_value, ('dp', 'mp'), 0, 0, tiled=True)  14.4 us
    unnamed x44, local copies, waits for them, and re-layouts  13.6 us
    all_to_all x1, starting transfers between devices, handoff(): lax.all_to_all(answer, 'mp', split_axis=0, concat_axis=0, tiled=True)  11.3 us
    ppermute x7, waiting for transfers between devices, moved_experts(): blocks.append(lax.ppermute(block, 'mp', chip_pairs(*shift)))  11.2 us
  transfers between devices with their start and end apart: 33, of which 9 were waited for; matrix products, arithmetic and copies ran while one was open for 9% of the time, Pallas kernels for 10%

commit v1 on v0

--- a/solution.py
+++ b/solution.py
@@ -54,7 +54,7 @@
             ready[part, :, :, columns] = picked.astype(ready.dtype).reshape(rows, slots, chunk)
             return carry
 
-        lax.fori_loop(0, width // chunk, step, 0)
+        lax.fori_loop(0, width // chunk, step, 0, unroll=True)
         outward[part].start()
     for copy in outward:
         copy.wait()
@@ -120,25 +120,26 @@
     return lax.dynamic_slice_in_dim(own, chip * rows, rows, axis=1)
 
 
-def moved_experts(own, inference_slot):
+def moved_experts(own, later, inference_slot):
     me = lax.axis_index("mp")
     chip = me // CORES
     z, x = chip // CHIPS_X, chip % CHIPS_X
     chips = Z_LO * CHIPS_X
     rows = own.shape[1] // chips
     sent = []
-    for dz, dx in SHIFTS:
+    for n, (dz, dx) in enumerate(SHIFTS):
         to = ((z + dz) % Z_LO) * CHIPS_X + (x + dx) % CHIPS_X
-        sent.append(chip_slice(own, to, rows))
+        sent.append(chip_slice(own if n < EARLY else later, to, rows))
+    mine = chip_slice(later, chip, rows)
     sent = lax.optimization_barrier(sent[:EARLY]) + lax.optimization_barrier(sent[EARLY:])
     blocks = []
     for shift, block in zip(SHIFTS, sent):
         blocks.append(lax.ppermute(block, "mp", chip_pairs(*shift)))
-    mine = chip_slice(own, chip, rows)
     swapped = []
     for block in [mine] + blocks:
         swapped.append(lax.ppermute(block, "mp", CORE_PAIRS))
-    me = passed_on(me[None].astype(jnp.int32))[0]
+    me = passed_on(me[None].astype(jnp.int32))
+    me = passed_on(me)[0]
     return placed_blocks(me, inference_slot, [mine] + blocks + swapped)
 
 
@@ -211,7 +212,7 @@
             pltpu.SemaphoreType.DMA((3,)),
             pltpu.SemaphoreType.DMA((width // 1024, count)),
         ],
-        compiler_params=pltpu.CompilerParams(vmem_limit_bytes=16 << 20),
+        compiler_params=pltpu.CompilerParams(vmem_limit_bytes=58 << 20),
         cost_estimate=pl.CostEstimate(flops=4 << 30, bytes_accessed=12 << 20, transcendentals=0),
         name="experts",
     )(*blocks, weights)
@@ -231,7 +232,7 @@
         groups.append([block])
         for dy in TURNS_Y:
             groups[-1].append(lax.ppermute(block, "dp", row_pairs(dy, 0)))
-    return groups[0] + groups[1]
+    return groups
 
 
 def added(blocks):
@@ -241,19 +242,11 @@
     return total.astype(jnp.bfloat16)
 
 
-def sums_at_owner(partials):
-    half = len(partials) // 2
-    sums = []
-    for turn in (1, 0):
-        blocks = partials[turn * half : (turn + 1) * half]
-        came = [blocks[0]]
-        for dy, block in zip(TURNS_Y, blocks[1:]):
-            came.append(lax.ppermute(block, "dp", row_pairs(-dy, 0)))
-        if turn:
-            sums.append(lax.ppermute(added(came), "dp", row_pairs(0, 1)))
-        else:
-            sums += came
-    return added(sums)
+def sums_along_y(partials):
+    came = [partials[0]]
+    for dy, block in zip(TURNS_Y, partials[1:]):
+        came.append(lax.ppermute(block, "dp", row_pairs(-dy, 0)))
+    return added(came)
 
 
 def handoff(
@@ -271,11 +264,12 @@
     )
     inference_slot = passed_on(inference_slot[None])[0]
     routes = passed_on(routes)
-    placed = moved_experts(expert_weights[0], inference_slot)
     column_width = attn_weight.shape[1]
     gathered = lax.all_to_all(
         jnp.broadcast_to(context[None], (dp_count, *context.shape)), "dp", 0, 0, tiled=True
     )
+    gathered, later = lax.optimization_barrier((gathered, expert_weights[0]))
+    placed = moved_experts(expert_weights[0], later, inference_slot)
     partial_value = jnp.dot(
         gathered.reshape(-1, context.shape[1]), attn_weight, preferred_element_type=jnp.float32
     ).astype(jnp.bfloat16)
@@ -316,12 +310,23 @@
         row_owner.T, placing * share.reshape(-1)[:, None], precision=lax.Precision.HIGHEST
     )
     own_rows = lax.all_to_all(outgoing, "mp", split_axis=0, concat_axis=0, tiled=True)
-    blocks = rows_of_all(own_rows.reshape(-1, model_width))
-    partials = expert_apply(blocks, expert_weights[0])
-    answer = sums_at_owner(partials).reshape(mp_count, capacity, model_width)
-    returned = lax.all_to_all(answer, "mp", split_axis=0, concat_axis=0, tiled=True)
+    groups = rows_of_all(own_rows.reshape(-1, model_width))
+    sums = []
+    for blocks in groups:
+        partials = expert_apply(blocks, expert_weights[0])
+        sums.append(sums_along_y(partials))
+    first = lax.axis_index("dp") % Z_HI == 0
+    answer = jnp.stack([jnp.where(first, sums[0], sums[1]), jnp.where(first, sums[1], sums[0])])
+    answer = answer.reshape(Z_HI * mp_count, capacity, model_width)
+    teams = [
+        [(y * Z_HI + z) * mp_count + m for z in range(Z_HI) for m in range(mp_count)]
+        for y in range(CHIPS_Y)
+    ]
+    returned = lax.all_to_all(
+        answer, ("dp", "mp"), 0, 0, axis_index_groups=teams, tiled=True
+    )
     expert_mix = jnp.dot(
-        combine_matrix,
+        jnp.concatenate([combine_matrix] * Z_HI, axis=1),
         returned.reshape(-1, model_width).astype(jnp.float32),
         precision=lax.Precision.HIGHEST,
     ).astype(jnp.bfloat16)

time: 209 us -> 219 us (1.048)
  waiting for transfers between devices: 59.6 us -> 80.3 us
  starting transfers between devices: 86.4 us -> 77.5 us
  Pallas kernels: 21.8 us -> 25.1 us
  local copies, waits for them, and re-layouts: 26.3 us -> 23.7 us
    ppermute x7, waiting for transfers between devices: 11.2 us -> 32.6 us  [moved_experts(): blocks.append(lax.ppermute(block, 'mp', chip_pairs(*shift)))]
    ppermute x7 -> x6, waiting for transfers between devices: 0.49 us -> 14.4 us  [sums_along_y(): came.append(lax.ppermute(block, 'dp', row_pairs(-dy, 0)))]
    ppermute x7 -> x6, starting transfers between devices: 18.2 us -> 5.72 us  [sums_along_y(): came.append(lax.ppermute(block, 'dp', row_pairs(-dy, 0)))]
    ppermute x8, starting transfers between devices: 15.1 us -> 27.2 us  [moved_experts(): swapped.append(lax.ppermute(block, 'mp', CORE_PAIRS))]
    ppermute x6, waiting for transfers between devices: 18.7 us -> 10.4 us  [rows_of_all(): groups[-1].append(lax.ppermute(block, 'dp', row_pairs(dy, 0)))]
    ppermute x7, starting transfers between devices: 14.9 us -> 7.28 us  [moved_experts(): blocks.append(lax.ppermute(block, 'mp', chip_pairs(*shift)))]
    all_to_all x1, waiting for transfers between devices: 7.02 us -> 0.29 us  [handoff(): lax.all_to_all(jnp.broadcast_to(context[None], (dp_count, *context.shape)...]
    unnamed x44, local copies, waits for them, and re-layouts: 13.6 us -> 6.9 us
  transfers between devices with their start and end apart: 33 -> 32, of which waited for: 9 -> 16; matrix products, arithmetic and copies ran while one was open for 9% -> 8% of each run, Pallas kernels for 10% -> 12%
where the time goes in v1:
time: 219 us; the launch traced here: 218 us
  waiting for transfers between devices  80.3 us (37%)
  starting transfers between devices  77.5 us (35%)
  Pallas kernels  25.1 us (11%)
  local copies, waits for them, and re-layouts  23.7 us (11%)
  other arithmetic  5.66 us (3%)
  between operations  3.5 us (2%)
  matrix products  2.65 us (1%)
    ppermute x7, waiting for transfers between devices, moved_experts(): blocks.append(lax.ppermute(block, 'mp', chip_pairs(*shift)))  32.6 us
    ppermute x8, starting transfers between devices, moved_experts(): swapped.append(lax.ppermute(block, 'mp', CORE_PAIRS))  27.2 us
    ppermute x6, waiting for transfers between devices, sums_along_y(): came.append(lax.ppermute(block, 'dp', row_pairs(-dy, 0)))  14.4 us
    pallas_call x2, Pallas kernels, expert_apply(): pl.pallas_call(functools.partial(expert_kernel, count), out_shape=[jax.Sh...  12.8 us
    all_to_all x1, waiting for transfers between devices, handoff(): summed = lax.all_to_all(partial_value, ('dp', 'mp'), 0, 0, tiled=True)  11.9 us
    ppermute x6, waiting for transfers between devices, rows_of_all(): groups[-1].append(lax.ppermute(block, 'dp', row_pairs(dy, 0)))  10.4 us
    all_to_all x1, starting transfers between devices, handoff(): summed = lax.all_to_all(partial_value, ('dp', 'mp'), 0, 0, tiled=True)  10.1 us
    all_to_all x1, starting transfers between devices, handoff(): lax.all_to_all(answer, ('dp', 'mp'), 0, 0, axis_index_groups=teams, tiled...  8.83 us
  transfers between devices with their start and end apart: 32, of which 16 were waited for; matrix products, arithmetic and copies ran while one was open for 8% of the time, Pallas kernels for 12%

profile of v1, /device:TPU:1, one launch (start us, length us, event | category | flops | bytes accessed | tf_op | source)
XLA Modules:
  0.0 218.5 jit_solution(8409541640052115396)
XLA Ops:
  0.6 1.7 broadcast_in_dim.48
  2.4 8.5 %all-to-all-start = ((bf16[8,64,512]{2,1,0:T(8,128)(2,1)}), bf16[8,64,512]{2,1,0:T(8,128)(2,1)S(1)}, u32[]{:S(2)}, u32[]{:S(2)}) async-start(bf16[8,64,512]{2,1,0:T(8,128)(2,1)} %broadcast_in_dim.48), calls=%async_computation | async-start | bytes 1048576 | tf_op jit(solution)/shard_map/all_to_all | solution.py:268
  11.4 1.2 shard_map.105
  14.9 0.7 select_reduce_fusion.5
  15.6 1.2 shard_map.106
  16.8 1.3 shard_map.103
  18.1 0.8 copy.11
  19.7 0.8 select_reduce_fusion.4
  21.1 0.6 convolution_convert_fusion.2
  21.6 1.0 reshape.148
  22.6 10.1 %all-to-all-start.1 = ((bf16[128,4,640]{2,1,0:T(4,128)(2,1)}), bf16[128,4,640]{2,1,0:T(4,128)(2,1)S(1)}, u32[]{:S(2)}, u32[]{:S(2)}) async-start(bf16[128,4,640]{2,1,0:T(4,128)(2,1)} %reshape.148), calls=%async_computation.1 | async-start | bytes 1310720 | tf_op jit(solution)/shard_map/all_to_all | solution.py:277
  32.9 3.0 %dynamic-slice_bitcast_fusion = (bf16[3,24,5120]{2,1,0:T(8,128)(2,1)}, bf16[3,24,5120]{2,1,0:T(8,128)(2,1)}, bf16[3,24,5120]{2,1,0:T(8,128)(2,1)}) fusion(bf16[1,3,192,5120]{3,2,1,0:T(8,128)(2,1)} %param.13, s32[]{:T(128)S(6)} %select_n.241, s32[]{:T(128)S(6)} %select_n.236, s32[]{:T(128)S(6)} %select_n.238), kind=kLoop, calls=%fused_computation.10 | loop fusion | bytes 4423692 | tf_op jit(solution)/shard_map/dynamic_slice | solution.py:120
  35.8 11.9 %all-to-all-done.1 = bf16[128,4,640]{2,1,0:T(4,128)(2,1)S(1)} async-done(((bf16[128,4,640]{2,1,0:T(4,128)(2,1)}), bf16[128,4,640]{2,1,0:T(4,128)(2,1)S(1)}, u32[]{:S(2)}, u32[]{:S(2)}) %all-to-all-start.1) | async-done | bytes 655392 | tf_op jit(solution)/shard_map/all_to_all | solution.py:277
  48.5 0.8 reshape.151
  49.4 4.3 %all-to-all-start.2 = ((bf16[16,2,5120]{2,1,0:T(2,128)(2,1)}), bf16[16,2,5120]{2,1,0:T(2,128)(2,1)S(1)}, u32[]{:S(2)}, u32[]{:S(2)}) async-start(bf16[16,2,5120]{2,1,0:T(2,128)(2,1)} %reshape.151), calls=%async_computation.2 | async-start | bytes 655360 | tf_op jit(solution)/shard_map/all_to_all | solution.py:312
  54.0 0.7 reshape.156.chooser
  54.7 6.7 %all-to-all-done.2 = bf16[16,2,5120]{2,1,0:T(2,128)(2,1)S(1)} async-done(((bf16[16,2,5120]{2,1,0:T(2,128)(2,1)}), bf16[16,2,5120]{2,1,0:T(2,128)(2,1)S(1)}, u32[]{:S(2)}, u32[]{:S(2)}) %all-to-all-start.2) | async-done | bytes 327712 | tf_op jit(solution)/shard_map/all_to_all | solution.py:312
  62.1 0.8 collective-permute-start.2
  62.9 1.9 collective-permute-start.1
  64.8 3.4 %constant_dynamic-slice_fusion.3 = (bf16[3,24,5120]{2,1,0:T(8,128)(2,1)S(1)}, bf16[3,24,5120]{2,1,0:T(8,128)(2,1)}, bf16[3,24,5120]{2,1,0:T(8,128)(2,1)}, bf16[3...) fusion(bf16[3,192,5120]{2,1,0:T(8,128)(2,1)} %bitcast.48, s32[]{:T(128)S(6)} %select_n.246, s32[]{:T(128)S(6)} %select_n.245, ...), kind=kLoop, calls=%fused_computation.54 | loop fusion | bytes 7372820 | tf_op jit(solution)/shard_map/dynamic_slice | solution.py:120
  68.2 3.2 %collective-permute-done.6.refs_0_ = bf16[32,5120]{1,0:T(8,128)(2,1)S(1)} collective-permute-done((bf16[32,5120]{1,0:T(8,128)(2,1)S(1)}, bf16[32,5120]{1,0:T(8,128)(2,1)S(1)}, u32[]{:S(2)}, u32[]{:S(2)}) %collective-permute-start.6) | collective-permute-done | bytes 327712 | tf_op jit(solution)/shard_map/ppermute | solution.py:229
  71.9 1.9 collective-permute-start.8
  73.8 4.9 %collective-permute-done.1.refs_2_ = bf16[32,5120]{1,0:T(8,128)(2,1)S(1)} collective-permute-done((bf16[32,5120]{1,0:T(8,128)(2,1)S(1)}, bf16[32,5120]{1,0:T(8,128)(2,1)S(1)}, u32[]{:S(2)}, u32[]{:S(2)}) %collective-permute-start.1) | collective-permute-done | bytes 327712 | tf_op jit(solution)/shard_map/ppermute | solution.py:234
  78.7 3.1 %collective-permute-done.refs_1_ = bf16[32,5120]{1,0:T(8,128)(2,1)S(1)} collective-permute-done((bf16[32,5120]{1,0:T(8,128)(2,1)S(1)}, bf16[32,5120]{1,0:T(8,128)(2,1)S(1)}, u32[]{:S(2)}, u32[]{:S(2)}) %collective-permute-start) | collective-permute-done | bytes 327712 | tf_op jit(solution)/shard_map/ppermute | solution.py:234
  81.8 0.7 copy-done.20
  82.5 6.4 %experts.2 = (bf16[32,5120]{1,0:T(8,128)(2,1)}, bf16[32,5120]{1,0:T(8,128)(2,1)}, bf16[32,5120]{1,0:T(8,128)(2,1)}, bf16[32,5120]{1,0:T(8,128)(2,1)}) custom-call(bf16[32,5120]{1,0:T(8,128)(2,1)} %copy-done.9, bf16[32,5120]{1,0:T(8,128)(2,1)} %copy-done.20, bf16[32,5120]{1,0:T(8,128)(2,1)} %copy-done.19, bf16[32,5120]{1,0:T(8,128)(2,1)} %copy-done.18, ...), custom_call_target="tpu_custom_call" | custom-call | flops 4294967296 | bytes 12582912 | tf_op jit(solution)/shard_map/experts/pallas_call | solution.py:202
  88.9 1.6 collective-permute-start.3
  90.6 1.3 collective-permute-start.5
  91.9 2.5 %collective-permute-done.7.refs_1_ = bf16[32,5120]{1,0:T(8,128)(2,1)} collective-permute-done((bf16[32,5120]{1,0:T(8,128)(2,1)S(1)}, bf16[32,5120]{1,0:T(8,128)(2,1)}, u32[]{:S(2)}, u32[]{:S(2)}) %collective-permute-start.7) | collective-permute-done | bytes 327712 | tf_op jit(solution)/shard_map/ppermute | solution.py:234
  94.4 6.4 %experts.3 = (bf16[32,5120]{1,0:T(8,128)(2,1)}, bf16[32,5120]{1,0:T(8,128)(2,1)}, bf16[32,5120]{1,0:T(8,128)(2,1)}, bf16[32,5120]{1,0:T(8,128)(2,1)}) custom-call(bf16[32,5120]{1,0:T(8,128)(2,1)} %copy-done.15, bf16[32,5120]{1,0:T(8,128)(2,1)} %collective-permute-done.7.refs_1_, bf16[32,5120]{1,0:T(8,128)(2,1)} %copy-done.17, bf16[32,5120]{1,0:T(8,128)(2,1)} %copy-done.16, ...), custom_call_target="tpu_custom_call" | custom-call | flops 4294967296 | bytes 12582912 | tf_op jit(solution)/shard_map/experts/pallas_call | solution.py:202
  100.8 1.5 collective-permute-start.10
  102.3 1.2 collective-permute-start.12
  104.0 0.7 collective-permute-start.13
  104.7 2.7 %collective-permute-done.5 = bf16[32,5120]{1,0:T(8,128)(2,1)} collective-permute-done((bf16[32,5120]{1,0:T(8,128)(2,1)}, bf16[32,5120]{1,0:T(8,128)(2,1)}, u32[]{:S(2)}, u32[]{:S(2)}) %collective-permute-start.5) | collective-permute-done | bytes 327712 | tf_op jit(solution)/shard_map/ppermute | solution.py:248
  107.4 1.9 collective-permute-start.14
  109.3 4.0 %collective-permute-done.10 = bf16[32,5120]{1,0:T(8,128)(2,1)S(1)} collective-permute-done((bf16[32,5120]{1,0:T(8,128)(2,1)}, bf16[32,5120]{1,0:T(8,128)(2,1)S(1)}, u32[]{:S(2)}, u32[]{:S(2)}) %collective-permute-start.10) | collective-permute-done | bytes 327712 | tf_op jit(solution)/shard_map/ppermute | solution.py:248
  113.6 3.2 %collective-permute-done.11 = bf16[32,5120]{1,0:T(8,128)(2,1)S(1)} collective-permute-done((bf16[32,5120]{1,0:T(8,128)(2,1)}, bf16[32,5120]{1,0:T(8,128)(2,1)S(1)}, u32[]{:S(2)}, u32[]{:S(2)}) %collective-permute-start.11) | collective-permute-done | bytes 327712 | tf_op jit(solution)/shard_map/ppermute | solution.py:248
  116.9 4.5 %collective-permute-done.12 = bf16[32,5120]{1,0:T(8,128)(2,1)S(1)} collective-permute-done((bf16[32,5120]{1,0:T(8,128)(2,1)}, bf16[32,5120]{1,0:T(8,128)(2,1)S(1)}, u32[]{:S(2)}, u32[]{:S(2)}) %collective-permute-start.12) | collective-permute-done | bytes 327712 | tf_op jit(solution)/shard_map/ppermute | solution.py:248
  121.4 1.3 collective-permute-start.17
  122.7 1.6 select_bitcast_fusion.1
  124.3 2.4 %collective-permute-start.18 = (bf16[3,24,5120]{2,1,0:T(8,128)(2,1)}, bf16[3,24,5120]{2,1,0:T(8,128)(2,1)}, u32[]{:S(2)}, u32[]{:S(2)}) collective-permute-start(bf16[3,24,5120]{2,1,0:T(8,128)(2,1)} %get-tuple-element.35), channel_id=1, source_target_pairs={{0,14},{1,15},{2,8},{3,9},{4,10},{5,11},{6,12},{7,13},{8,6},{9,7},... | collective-permute-start | bytes 2211848 | tf_op jit(solution)/shard_map/ppermute | solution.py:137
  126.7 0.7 collective-permute-start.19
  127.3 2.0 collective-permute-done.15.refs_3_
  129.4 11.6 %collective-permute-start.20 = (bf16[3,24,5120]{2,1,0:T(8,128)(2,1)S(1)}, bf16[3,24,5120]{2,1,0:T(8,128)(2,1)S(1)}, u32[]{:S(2)}, u32[]{:S(2)}) collective-permute-start(bf16[3,24,5120]{2,1,0:T(8,128)(2,1)S(1)} %get-tuple-element.48.refs_0_), channel_id=1, source_target_pairs={{0,1},{1,0},{2,3},{3,2},{4,5},{5,4},{6,7},{7,6},{8,9},{9,8},{10,11... | collective-permute-start | bytes 2211848 | tf_op jit(solution)/shard_map/ppermute | solution.py:140
  140.9 3.4 %collective-permute-start.21 = (bf16[3,24,5120]{2,1,0:T(8,128)(2,1)S(1)}, bf16[3,24,5120]{2,1,0:T(8,128)(2,1)S(1)}, u32[]{:S(2)}, u32[]{:S(2)}) collective-permute-start(bf16[3,24,5120]{2,1,0:T(8,128)(2,1)S(1)} %collective-permute-done.13.refs_1_), channel_id=1, source_target_pairs={{0,1},{1,0},{2,3},{3,2},{4,5},{5,4},{6,7},{7,6},{8,9},{9,8},{10,11... | collective-permute-start | bytes 2211848 | tf_op jit(solution)/shard_map/ppermute | solution.py:140
  144.3 19.0 %collective-permute-done.17.refs_5_ = bf16[3,24,5120]{2,1,0:T(8,128)(2,1)} collective-permute-done((bf16[3,24,5120]{2,1,0:T(8,128)(2,1)}, bf16[3,24,5120]{2,1,0:T(8,128)(2,1)}, u32[]{:S(2)}, u32[]{:S(2)}) %collective-permute-start.17) | collective-permute-done | bytes 737312 | tf_op jit(solution)/shard_map/ppermute | solution.py:137
  163.3 1.7 collective-permute-start.22
  165.0 4.7 %collective-permute-done.18.refs_6_ = bf16[3,24,5120]{2,1,0:T(8,128)(2,1)} collective-permute-done((bf16[3,24,5120]{2,1,0:T(8,128)(2,1)}, bf16[3,24,5120]{2,1,0:T(8,128)(2,1)}, u32[]{:S(2)}, u32[]{:S(2)}) %collective-permute-start.18) | collective-permute-done | bytes 737312 | tf_op jit(solution)/shard_map/ppermute | solution.py:137
  169.7 7.1 %collective-permute-start.23 = (bf16[3,24,5120]{2,1,0:T(8,128)(2,1)}, bf16[3,24,5120]{2,1,0:T(8,128)(2,1)}, u32[]{:S(2)}, u32[]{:S(2)}) collective-permute-start(bf16[3,24,5120]{2,1,0:T(8,128)(2,1)} %collective-permute-done.15.refs_3_), channel_id=1, source_target_pairs={{0,1},{1,0},{2,3},{3,2},{4,5},{5,4},{6,7},{7,6},{8,9},{9,8},{10,11... | collective-permute-start | bytes 2211848 | tf_op jit(solution)/shard_map/ppermute | solution.py:140
  176.9 6.8 %collective-permute-done.19.refs_7_ = bf16[3,24,5120]{2,1,0:T(8,128)(2,1)} collective-permute-done((bf16[3,24,5120]{2,1,0:T(8,128)(2,1)S(1)}, bf16[3,24,5120]{2,1,0:T(8,128)(2,1)}, u32[]{:S(2)}, u32[]{:S(2)}) %collective-permute-start.19) | collective-permute-done | bytes 737312 | tf_op jit(solution)/shard_map/ppermute | solution.py:137
  183.7 3.0 %collective-permute-start.24 = (bf16[3,24,5120]{2,1,0:T(8,128)(2,1)}, bf16[3,24,5120]{2,1,0:T(8,128)(2,1)}, u32[]{:S(2)}, u32[]{:S(2)}) collective-permute-start(bf16[3,24,5120]{2,1,0:T(8,128)(2,1)} %collective-permute-done.16.refs_4_), channel_id=1, source_target_pairs={{0,1},{1,0},{2,3},{3,2},{4,5},{5,4},{6,7},{7,6},{8,9},{9,8},{10,11... | collective-permute-start | bytes 2211848 | tf_op jit(solution)/shard_map/ppermute | solution.py:140
  186.7 0.9 copy-done.1
  187.6 0.9 copy-done.3
  189.0 0.9 copy-done.5
  190.0 0.9 pad_maximum_fusion
  190.9 2.7 %reshape.153 = bf16[32,2,5120]{2,1,0:T(2,128)(2,1)} reshape(bf16[2,32,5120]{2,1,0:T(8,128)(2,1)} %pad_maximum_fusion) | data formatting | bytes 1310720 | tf_op jit(solution)/shard_map/reshape | solution.py:320
  193.6 8.8 %all-to-all-start.3 = ((bf16[32,2,5120]{2,1,0:T(2,128)(2,1)}), bf16[32,2,5120]{2,1,0:T(2,128)(2,1)}, u32[]{:S(2)}, u32[]{:S(2)}) async-start(bf16[32,2,5120]{2,1,0:T(2,128)(2,1)} %reshape.153), calls=%async_computation.3 | async-start | bytes 1310720 | tf_op jit(solution)/shard_map/all_to_all | solution.py:325
  202.9 1.1 copy-done.2
  204.0 1.1 copy-done.4
  205.2 1.1 copy-done.6
  206.3 8.3 %placing.1 = bf16[3,12,16,5120]{3,2,1,0:T(8,128)(2,1)} custom-call(s32[1]{0:T(128)} %bitcast.8.meta, bf16[192,256]{1,0:T(8,128)(2,1)S(1)} %reshape.156.chooser, bf16[3,24,5120]{2,1,0:T(8,128)(2,1)S(1)} %get-tuple-element.48.refs_0_, bf16[3,24,5120]{2,1,0:T(8,128)(2,1)S(1)} %collective-permute-done.13.refs_1_, ...), custom_call_target="tpu_custom_call" | custom-call | flops 2147483648 | bytes 16777216 | tf_op jit(solution)/shard_map/placing/pallas_call | solution.py:82
  214.6 0.8 all-to-all-done.3
  215.3 2.1 reshape.154
  217.4 1.1 convolution_convert_fusion.1
  (91 shorter events, 6.1 us)
Async XLA Ops:
  0.6 20.4 %copy-start = (bf16[512,640]{1,0:T(8,128)(2,1)S(1)}, bf16[512,640]{1,0:T(8,128)(2,1)}, u32[]{:S(2)}) copy-start(bf16[512,640]{1,0:T(8,128)(2,1)} %param.9) | copy-start | bytes 1966084
  2.4 45.6 %copy-start.13 = (bf16[4,5120]{1,0:T(4,128)(2,1)S(1)}, bf16[4,5120]{1,0:T(4,128)(2,1)}, u32[]{:S(2)}) copy-start(bf16[4,5120]{1,0:T(4,128)(2,1)} %param.10) | copy-start | bytes 122884
  2.4 45.8 %copy-start.14 = (f32[5120]{0:T(1024)S(1)}, f32[5120]{0:T(1024)}, u32[]{:S(2)}) copy-start(f32[5120]{0:T(1024)} %param.11) | copy-start | bytes 61444
  2.4 18.7 %all-to-all-start = ((bf16[8,64,512]{2,1,0:T(8,128)(2,1)}), bf16[8,64,512]{2,1,0:T(8,128)(2,1)S(1)}, u32[]{:S(2)}, u32[]{:S(2)}) async-start(bf16[8,64,512]{2,1,0:T(8,128)(2,1)} %broadcast_in_dim.48), calls=%async_computation | async-start | bytes 1048576 | tf_op jit(solution)/shard_map/all_to_all | solution.py:268
  22.6 25.1 %all-to-all-start.1 = ((bf16[128,4,640]{2,1,0:T(4,128)(2,1)}), bf16[128,4,640]{2,1,0:T(4,128)(2,1)S(1)}, u32[]{:S(2)}, u32[]{:S(2)}) async-start(bf16[128,4,640]{2,1,0:T(4,128)(2,1)} %reshape.148), calls=%async_computation.1 | async-start | bytes 1310720 | tf_op jit(solution)/shard_map/all_to_all | solution.py:277
  48.2 55.4 %copy-start.12 = (bf16[4,5120]{1,0:T(4,128)(2,1)}, bf16[4,5120]{1,0:T(4,128)(2,1)S(1)}, u32[]{:S(2)}) copy-start(bf16[4,5120]{1,0:T(4,128)(2,1)S(1)} %get-tuple-element.43) | copy-start | bytes 122884
  49.4 12.0 %all-to-all-start.2 = ((bf16[16,2,5120]{2,1,0:T(2,128)(2,1)}), bf16[16,2,5120]{2,1,0:T(2,128)(2,1)S(1)}, u32[]{:S(2)}, u32[]{:S(2)}) async-start(bf16[16,2,5120]{2,1,0:T(2,128)(2,1)} %reshape.151), calls=%async_computation.2 | async-start | bytes 655360 | tf_op jit(solution)/shard_map/all_to_all | solution.py:312
  61.5 20.2 %copy-start.9 = (bf16[32,5120]{1,0:T(8,128)(2,1)}, bf16[32,5120]{1,0:T(8,128)(2,1)S(1)}, u32[]{:S(2)}) copy-start(bf16[32,5120]{1,0:T(8,128)(2,1)S(1)} %reshape.152.refs_0_) | copy-start | bytes 983044
  61.5 9.9 %collective-permute-start.6 = (bf16[32,5120]{1,0:T(8,128)(2,1)S(1)}, bf16[32,5120]{1,0:T(8,128)(2,1)S(1)}, u32[]{:S(2)}, u32[]{:S(2)}) collective-permute-start(bf16[32,5120]{1,0:T(8,128)(2,1)S(1)} %reshape.152.refs_0_), channel_id=1, source_target_pairs={{0,16},{16,0},{32,48},{48,32},{64,80},{80,64},{96,112},{112,96},{1... | collective-permute-start | bytes 983048 | tf_op jit(solution)/shard_map/ppermute | solution.py:229
  62.1 11.7 %collective-permute-start.2 = (bf16[32,5120]{1,0:T(8,128)(2,1)S(1)}, bf16[32,5120]{1,0:T(8,128)(2,1)S(1)}, u32[]{:S(2)}, u32[]{:S(2)}) collective-permute-start(bf16[32,5120]{1,0:T(8,128)(2,1)S(1)} %reshape.152.refs_0_), channel_id=1, source_target_pairs={{0,64},{16,80},{32,96},{48,112},{64,0},{80,16},{96,32},{112,48},{1... | collective-permute-start | bytes 983048 | tf_op jit(solution)/shard_map/ppermute | solution.py:234
  62.9 15.8 %collective-permute-start.1 = (bf16[32,5120]{1,0:T(8,128)(2,1)S(1)}, bf16[32,5120]{1,0:T(8,128)(2,1)S(1)}, u32[]{:S(2)}, u32[]{:S(2)}) collective-permute-start(bf16[32,5120]{1,0:T(8,128)(2,1)S(1)} %reshape.152.refs_0_), channel_id=1, source_target_pairs={{0,96},{16,112},{32,0},{48,16},{64,32},{80,48},{96,64},{112,80},{1... | collective-permute-start | bytes 983048 | tf_op jit(solution)/shard_map/ppermute | solution.py:234
  64.8 16.9 %collective-permute-start = (bf16[32,5120]{1,0:T(8,128)(2,1)S(1)}, bf16[32,5120]{1,0:T(8,128)(2,1)S(1)}, u32[]{:S(2)}, u32[]{:S(2)}) collective-permute-start(bf16[32,5120]{1,0:T(8,128)(2,1)S(1)} %reshape.152.refs_0_), channel_id=1, source_target_pairs={{0,32},{16,48},{32,64},{48,80},{64,96},{80,112},{96,0},{112,16},{1... | collective-permute-start | bytes 983048 | tf_op jit(solution)/shard_map/ppermute | solution.py:234
  71.4 17.4 %copy-start.15 = (bf16[32,5120]{1,0:T(8,128)(2,1)}, bf16[32,5120]{1,0:T(8,128)(2,1)S(1)}, u32[]{:S(2)}) copy-start(bf16[32,5120]{1,0:T(8,128)(2,1)S(1)} %collective-permute-done.6.refs_0_) | copy-start | bytes 983044
  71.5 19.1 %collective-permute-start.9 = (bf16[32,5120]{1,0:T(8,128)(2,1)S(1)}, bf16[32,5120]{1,0:T(8,128)(2,1)S(1)}, u32[]{:S(2)}, u32[]{:S(2)}) collective-permute-start(bf16[32,5120]{1,0:T(8,128)(2,1)S(1)} %collective-permute-done.6.refs_0_), channel_id=1, source_target_pairs={{0,64},{16,80},{32,96},{48,112},{64,0},{80,16},{96,32},{112,48},{1... | collective-permute-start | bytes 983048 | tf_op jit(solution)/shard_map/ppermute | solution.py:234
  71.9 20.0 %collective-permute-start.8 = (bf16[32,5120]{1,0:T(8,128)(2,1)S(1)}, bf16[32,5120]{1,0:T(8,128)(2,1)S(1)}, u32[]{:S(2)}, u32[]{:S(2)}) collective-permute-start(bf16[32,5120]{1,0:T(8,128)(2,1)S(1)} %collective-permute-done.6.refs_0_), channel_id=1, source_target_pairs={{0,96},{16,112},{32,0},{48,16},{64,32},{80,48},{96,64},{112,80},{1... | collective-permute-start | bytes 983048 | tf_op jit(solution)/shard_map/ppermute | solution.py:234
  73.8 8.0 %copy-start.18 = (bf16[32,5120]{1,0:T(8,128)(2,1)}, bf16[32,5120]{1,0:T(8,128)(2,1)S(1)}, u32[]{:S(2)}) copy-start(bf16[32,5120]{1,0:T(8,128)(2,1)S(1)} %collective-permute-done.2.refs_3_) | copy-start | bytes 983044
  73.8 20.6 %collective-permute-start.7 = (bf16[32,5120]{1,0:T(8,128)(2,1)S(1)}, bf16[32,5120]{1,0:T(8,128)(2,1)}, u32[]{:S(2)}, u32[]{:S(2)}) collective-permute-start(bf16[32,5120]{1,0:T(8,128)(2,1)S(1)} %collective-permute-done.6.refs_0_), channel_id=1, source_target_pairs={{0,32},{16,48},{32,64},{48,80},{64,96},{80,112},{96,0},{112,16},{1... | collective-permute-start | bytes 983048 | tf_op jit(solution)/shard_map/ppermute | solution.py:234
  78.7 3.1 %copy-start.19 = (bf16[32,5120]{1,0:T(8,128)(2,1)}, bf16[32,5120]{1,0:T(8,128)(2,1)S(1)}, u32[]{:S(2)}) copy-start(bf16[32,5120]{1,0:T(8,128)(2,1)S(1)} %collective-permute-done.1.refs_2_) | copy-start | bytes 983044
  81.8 0.7 copy-start.20
  88.9 13.4 %collective-permute-start.3 = (bf16[32,5120]{1,0:T(8,128)(2,1)}, bf16[32,5120]{1,0:T(8,128)(2,1)S(1)}, u32[]{:S(2)}, u32[]{:S(2)}) collective-permute-start(bf16[32,5120]{1,0:T(8,128)(2,1)} %get-tuple-element.22), channel_id=1, source_target_pairs={{0,96},{16,112},{32,0},{48,16},{64,32},{80,48},{96,64},{112,80},{1... | collective-permute-start | bytes 983048 | tf_op jit(solution)/shard_map/ppermute | solution.py:248
  90.5 13.5 %collective-permute-start.4 = (bf16[32,5120]{1,0:T(8,128)(2,1)}, bf16[32,5120]{1,0:T(8,128)(2,1)}, u32[]{:S(2)}, u32[]{:S(2)}) collective-permute-start(bf16[32,5120]{1,0:T(8,128)(2,1)} %get-tuple-element.23), channel_id=1, source_target_pairs={{0,32},{16,48},{32,64},{48,80},{64,96},{80,112},{96,0},{112,16},{1... | collective-permute-start | bytes 983048 | tf_op jit(solution)/shard_map/ppermute | solution.py:248
  90.5 3.9 %copy-start.16 = (bf16[32,5120]{1,0:T(8,128)(2,1)}, bf16[32,5120]{1,0:T(8,128)(2,1)S(1)}, u32[]{:S(2)}) copy-start(bf16[32,5120]{1,0:T(8,128)(2,1)S(1)} %collective-permute-done.9.refs_3_) | copy-start | bytes 983044
  90.5 13.0 %copy-start.21 = (bf16[16,5120]{1,0:T(8,128)(2,1)S(1)}, bf16[16,5120]{1,0:T(8,128)(2,1)}, u32[]{:S(2)}) copy-start(bf16[16,5120]{1,0:T(8,128)(2,1)} %param.12) | copy-start | bytes 491524
  90.5 16.9 %copy-start.8 = (bf16[3,24,5120]{2,1,0:T(8,128)(2,1)S(1)}, bf16[3,24,5120]{2,1,0:T(8,128)(2,1)}, u32[]{:S(2)}) copy-start(bf16[3,24,5120]{2,1,0:T(8,128)(2,1)} %get-tuple-element.31) | copy-start | bytes 2211844
  90.5 22.8 %copy-start.7 = (bf16[3,24,5120]{2,1,0:T(8,128)(2,1)S(1)}, bf16[3,24,5120]{2,1,0:T(8,128)(2,1)}, u32[]{:S(2)}) copy-start(bf16[3,24,5120]{2,1,0:T(8,128)(2,1)} %get-tuple-element.32) | copy-start | bytes 2211844
  90.5 32.1 %copy-start.10 = (bf16[32,5120]{1,0:T(8,128)(2,1)S(1)}, bf16[32,5120]{1,0:T(8,128)(2,1)}, u32[]{:S(2)}) copy-start(bf16[32,5120]{1,0:T(8,128)(2,1)} %get-tuple-element.21) | copy-start | bytes 983044
  90.6 16.9 %collective-permute-start.5 = (bf16[32,5120]{1,0:T(8,128)(2,1)}, bf16[32,5120]{1,0:T(8,128)(2,1)}, u32[]{:S(2)}, u32[]{:S(2)}) collective-permute-start(bf16[32,5120]{1,0:T(8,128)(2,1)} %get-tuple-element.24), channel_id=1, source_target_pairs={{0,64},{16,80},{32,96},{48,112},{64,0},{80,16},{96,32},{112,48},{1... | collective-permute-start | bytes 983048 | tf_op jit(solution)/shard_map/ppermute | solution.py:248
  91.9 2.5 %copy-start.17 = (bf16[32,5120]{1,0:T(8,128)(2,1)}, bf16[32,5120]{1,0:T(8,128)(2,1)S(1)}, u32[]{:S(2)}) copy-start(bf16[32,5120]{1,0:T(8,128)(2,1)S(1)} %collective-permute-done.8.refs_2_) | copy-start | bytes 983044
  100.8 12.5 %collective-permute-start.10 = (bf16[32,5120]{1,0:T(8,128)(2,1)}, bf16[32,5120]{1,0:T(8,128)(2,1)S(1)}, u32[]{:S(2)}, u32[]{:S(2)}) collective-permute-start(bf16[32,5120]{1,0:T(8,128)(2,1)} %get-tuple-element.26), channel_id=1, source_target_pairs={{0,96},{16,112},{32,0},{48,16},{64,32},{80,48},{96,64},{112,80},{1... | collective-permute-start | bytes 983048 | tf_op jit(solution)/shard_map/ppermute | solution.py:248
  102.3 14.6 %collective-permute-start.11 = (bf16[32,5120]{1,0:T(8,128)(2,1)}, bf16[32,5120]{1,0:T(8,128)(2,1)S(1)}, u32[]{:S(2)}, u32[]{:S(2)}) collective-permute-start(bf16[32,5120]{1,0:T(8,128)(2,1)} %get-tuple-element.27), channel_id=1, source_target_pairs={{0,32},{16,48},{32,64},{48,80},{64,96},{80,112},{96,0},{112,16},{1... | collective-permute-start | bytes 983048 | tf_op jit(solution)/shard_map/ppermute | solution.py:248
  102.3 20.4 %copy-start.11 = (bf16[32,5120]{1,0:T(8,128)(2,1)}, bf16[32,5120]{1,0:T(8,128)(2,1)S(1)}, u32[]{:S(2)}) copy-start(bf16[32,5120]{1,0:T(8,128)(2,1)S(1)} %collective-permute-done.3) | copy-start | bytes 983044
  102.3 19.1 %collective-permute-start.12 = (bf16[32,5120]{1,0:T(8,128)(2,1)}, bf16[32,5120]{1,0:T(8,128)(2,1)S(1)}, u32[]{:S(2)}, u32[]{:S(2)}) collective-permute-start(bf16[32,5120]{1,0:T(8,128)(2,1)} %get-tuple-element.28), channel_id=1, source_target_pairs={{0,64},{16,80},{32,96},{48,112},{64,0},{80,16},{96,32},{112,48},{1... | collective-permute-start | bytes 983048 | tf_op jit(solution)/shard_map/ppermute | solution.py:248
  104.0 20.3 %collective-permute-start.13 = (bf16[3,24,5120]{2,1,0:T(8,128)(2,1)}, bf16[3,24,5120]{2,1,0:T(8,128)(2,1)S(1)}, u32[]{:S(2)}, u32[]{:S(2)}) collective-permute-start(bf16[3,24,5120]{2,1,0:T(8,128)(2,1)} %get-tuple-element.30), channel_id=1, source_target_pairs={{0,2},{1,3},{2,4},{3,5},{4,6},{5,7},{6,0},{7,1},{8,10},{9,11},{10,... | collective-permute-start | bytes 2211848 | tf_op jit(solution)/shard_map/ppermute | solution.py:137
  107.4 19.3 %collective-permute-start.14 = (bf16[3,24,5120]{2,1,0:T(8,128)(2,1)S(1)}, bf16[3,24,5120]{2,1,0:T(8,128)(2,1)S(1)}, u32[]{:S(2)}, u32[]{:S(2)}) collective-permute-start(bf16[3,24,5120]{2,1,0:T(8,128)(2,1)S(1)} %copy-done.8), channel_id=1, source_target_pairs={{0,6},{1,7},{2,0},{3,1},{4,2},{5,3},{6,4},{7,5},{8,14},{9,15},{10,... | collective-permute-start | bytes 2211848 | tf_op jit(solution)/shard_map/ppermute | solution.py:137
  113.3 16.1 %collective-permute-start.15 = (bf16[3,24,5120]{2,1,0:T(8,128)(2,1)S(1)}, bf16[3,24,5120]{2,1,0:T(8,128)(2,1)}, u32[]{:S(2)}, u32[]{:S(2)}) collective-permute-start(bf16[3,24,5120]{2,1,0:T(8,128)(2,1)S(1)} %copy-done.7), channel_id=1, source_target_pairs={{0,8},{1,9},{2,10},{3,11},{4,12},{5,13},{6,14},{7,15},{8,0},{9,1},... | collective-permute-start | bytes 2211848 | tf_op jit(solution)/shard_map/ppermute | solution.py:137
  116.8 24.1 %collective-permute-start.16 = (bf16[3,24,5120]{2,1,0:T(8,128)(2,1)}, bf16[3,24,5120]{2,1,0:T(8,128)(2,1)}, u32[]{:S(2)}, u32[]{:S(2)}) collective-permute-start(bf16[3,24,5120]{2,1,0:T(8,128)(2,1)} %get-tuple-element.33), channel_id=1, source_target_pairs={{0,4},{1,5},{2,6},{3,7},{4,0},{5,1},{6,2},{7,3},{8,12},{9,13},{10,... | collective-permute-start | bytes 2211848 | tf_op jit(solution)/shard_map/ppermute | solution.py:137
  121.4 41.9 %collective-permute-start.17 = (bf16[3,24,5120]{2,1,0:T(8,128)(2,1)}, bf16[3,24,5120]{2,1,0:T(8,128)(2,1)}, u32[]{:S(2)}, u32[]{:S(2)}) collective-permute-start(bf16[3,24,5120]{2,1,0:T(8,128)(2,1)} %get-tuple-element.34), channel_id=1, source_target_pairs={{0,10},{1,11},{2,12},{3,13},{4,14},{5,15},{6,8},{7,9},{8,2},{9,3},... | collective-permute-start | bytes 2211848 | tf_op jit(solution)/shard_map/ppermute | solution.py:137
  124.3 45.4 %collective-permute-start.18 = (bf16[3,24,5120]{2,1,0:T(8,128)(2,1)}, bf16[3,24,5120]{2,1,0:T(8,128)(2,1)}, u32[]{:S(2)}, u32[]{:S(2)}) collective-permute-start(bf16[3,24,5120]{2,1,0:T(8,128)(2,1)} %get-tuple-element.35), channel_id=1, source_target_pairs={{0,14},{1,15},{2,8},{3,9},{4,10},{5,11},{6,12},{7,13},{8,6},{9,7},... | collective-permute-start | bytes 2211848 | tf_op jit(solution)/shard_map/ppermute | solution.py:137
  126.7 57.0 %collective-permute-start.19 = (bf16[3,24,5120]{2,1,0:T(8,128)(2,1)S(1)}, bf16[3,24,5120]{2,1,0:T(8,128)(2,1)}, u32[]{:S(2)}, u32[]{:S(2)}) collective-permute-start(bf16[3,24,5120]{2,1,0:T(8,128)(2,1)S(1)} %get-tuple-element.36), channel_id=1, source_target_pairs={{0,12},{1,13},{2,14},{3,15},{4,8},{5,9},{6,10},{7,11},{8,4},{9,5},... | collective-permute-start | bytes 2211848 | tf_op jit(solution)/shard_map/ppermute | solution.py:137
  129.4 57.4 %collective-permute-start.20 = (bf16[3,24,5120]{2,1,0:T(8,128)(2,1)S(1)}, bf16[3,24,5120]{2,1,0:T(8,128)(2,1)S(1)}, u32[]{:S(2)}, u32[]{:S(2)}) collective-permute-start(bf16[3,24,5120]{2,1,0:T(8,128)(2,1)S(1)} %get-tuple-element.48.refs_0_), channel_id=1, source_target_pairs={{0,1},{1,0},{2,3},{3,2},{4,5},{5,4},{6,7},{7,6},{8,9},{9,8},{10,11... | collective-permute-start | bytes 2211848 | tf_op jit(solution)/shard_map/ppermute | solution.py:140
  140.9 46.7 %collective-permute-start.21 = (bf16[3,24,5120]{2,1,0:T(8,128)(2,1)S(1)}, bf16[3,24,5120]{2,1,0:T(8,128)(2,1)S(1)}, u32[]{:S(2)}, u32[]{:S(2)}) collective-permute-start(bf16[3,24,5120]{2,1,0:T(8,128)(2,1)S(1)} %collective-permute-done.13.refs_1_), channel_id=1, source_target_pairs={{0,1},{1,0},{2,3},{3,2},{4,5},{5,4},{6,7},{7,6},{8,9},{9,8},{10,11... | collective-permute-start | bytes 2211848 | tf_op jit(solution)/shard_map/ppermute | solution.py:140
  163.3 25.7 %collective-permute-start.22 = (bf16[3,24,5120]{2,1,0:T(8,128)(2,1)S(1)}, bf16[3,24,5120]{2,1,0:T(8,128)(2,1)S(1)}, u32[]{:S(2)}, u32[]{:S(2)}) collective-permute-start(bf16[3,24,5120]{2,1,0:T(8,128)(2,1)S(1)} %collective-permute-done.14.refs_2_), channel_id=1, source_target_pairs={{0,1},{1,0},{2,3},{3,2},{4,5},{5,4},{6,7},{7,6},{8,9},{9,8},{10,11... | collective-permute-start | bytes 2211848 | tf_op jit(solution)/shard_map/ppermute | solution.py:140
  169.7 33.1 %collective-permute-start.23 = (bf16[3,24,5120]{2,1,0:T(8,128)(2,1)}, bf16[3,24,5120]{2,1,0:T(8,128)(2,1)}, u32[]{:S(2)}, u32[]{:S(2)}) collective-permute-start(bf16[3,24,5120]{2,1,0:T(8,128)(2,1)} %collective-permute-done.15.refs_3_), channel_id=1, source_target_pairs={{0,1},{1,0},{2,3},{3,2},{4,5},{5,4},{6,7},{7,6},{8,9},{9,8},{10,11... | collective-permute-start | bytes 2211848 | tf_op jit(solution)/shard_map/ppermute | solution.py:140
  183.7 19.2 %collective-permute-start.24 = (bf16[3,24,5120]{2,1,0:T(8,128)(2,1)}, bf16[3,24,5120]{2,1,0:T(8,128)(2,1)}, u32[]{:S(2)}, u32[]{:S(2)}) collective-permute-start(bf16[3,24,5120]{2,1,0:T(8,128)(2,1)} %collective-permute-done.16.refs_4_), channel_id=1, source_target_pairs={{0,1},{1,0},{2,3},{3,2},{4,5},{5,4},{6,7},{7,6},{8,9},{9,8},{10,11... | collective-permute-start | bytes 2211848 | tf_op jit(solution)/shard_map/ppermute | solution.py:140
  186.7 0.9 copy-start.1
  187.6 15.3 %collective-permute-start.25 = (bf16[3,24,5120]{2,1,0:T(8,128)(2,1)}, bf16[3,24,5120]{2,1,0:T(8,128)(2,1)}, u32[]{:S(2)}, u32[]{:S(2)}) collective-permute-start(bf16[3,24,5120]{2,1,0:T(8,128)(2,1)} %collective-permute-done.17.refs_5_), channel_id=1, source_target_pairs={{0,1},{1,0},{2,3},{3,2},{4,5},{5,4},{6,7},{7,6},{8,9},{9,8},{10,11... | collective-permute-start | bytes 2211848 | tf_op jit(solution)/shard_map/ppermute | solution.py:140
  187.6 0.9 copy-start.3
  188.5 14.4 %collective-permute-start.26 = (bf16[3,24,5120]{2,1,0:T(8,128)(2,1)}, bf16[3,24,5120]{2,1,0:T(8,128)(2,1)}, u32[]{:S(2)}, u32[]{:S(2)}) collective-permute-start(bf16[3,24,5120]{2,1,0:T(8,128)(2,1)} %collective-permute-done.18.refs_6_), channel_id=1, source_target_pairs={{0,1},{1,0},{2,3},{3,2},{4,5},{5,4},{6,7},{7,6},{8,9},{9,8},{10,11... | collective-permute-start | bytes 2211848 | tf_op jit(solution)/shard_map/ppermute | solution.py:140
  189.0 0.9 copy-start.5
  190.0 12.9 %collective-permute-start.27 = (bf16[3,24,5120]{2,1,0:T(8,128)(2,1)}, bf16[3,24,5120]{2,1,0:T(8,128)(2,1)}, u32[]{:S(2)}, u32[]{:S(2)}) collective-permute-start(bf16[3,24,5120]{2,1,0:T(8,128)(2,1)} %collective-permute-done.19.refs_7_), channel_id=1, source_target_pairs={{0,1},{1,0},{2,3},{3,2},{4,5},{5,4},{6,7},{7,6},{8,9},{9,8},{10,11... | collective-permute-start | bytes 2211848 | tf_op jit(solution)/shard_map/ppermute | solution.py:140
  193.6 21.7 %all-to-all-start.3 = ((bf16[32,2,5120]{2,1,0:T(2,128)(2,1)}), bf16[32,2,5120]{2,1,0:T(2,128)(2,1)}, u32[]{:S(2)}, u32[]{:S(2)}) async-start(bf16[32,2,5120]{2,1,0:T(2,128)(2,1)} %reshape.153), calls=%async_computation.3 | async-start | bytes 1310720 | tf_op jit(solution)/shard_map/all_to_all | solution.py:325
  202.9 1.1 copy-start.2
  204.0 1.1 copy-start.4
  205.2 1.1 copy-start.6

commit v2 on v1

--- a/solution.py
+++ b/solution.py
@@ -26,7 +26,7 @@
 CORE_PAIRS = [(i, i ^ 1) for i in range(Z_LO * CHIPS_X * CORES)]
 
 
-def placing_kernel(count, meta, chooser, *refs):
+def placing_kernel(count, meta, goes, *refs):
     blocks, out = refs[:count], refs[count]
     held, ready, in_sem, out_sem = refs[count + 1 :]
     parts, rows, slots, width = ready.shape
@@ -38,6 +38,14 @@
             copies.append(pltpu.make_async_copy(ref, held.at[part, k], in_sem.at[part, k]))
     for copy in copies:
         copy.start()
+    column = lax.broadcasted_iota(jnp.int32, (rows * slots, count * 16), 1)
+    line = lax.broadcasted_iota(jnp.int32, (rows * slots, count * 16), 0)
+    target = jnp.zeros_like(column)
+    for k in range(count):
+        target = jnp.where(column // 16 == k, goes[k], target)
+    chooser = (
+        (line // slots + 4 * lax.rem(meta[0], CORES) == column % 16) & (line % slots == target)
+    ).astype(ready.dtype)
     outward = [
         pltpu.make_async_copy(ready.at[part], out.at[part], out_sem.at[part])
         for part in range(parts)
@@ -50,7 +58,7 @@
         def step(at, carry, part=part):
             columns = pl.ds(pl.multiple_of(at * chunk, chunk), chunk)
             block = held[part, :, :, columns].reshape(count * 16, chunk)
-            picked = jnp.dot(chooser[...], block, preferred_element_type=jnp.float32)
+            picked = jnp.dot(chooser, block, preferred_element_type=jnp.float32)
             ready[part, :, :, columns] = picked.astype(ready.dtype).reshape(rows, slots, chunk)
             return carry
 
@@ -74,17 +82,13 @@
     came = jnp.stack(came)
     ids = jnp.arange(slots, dtype=jnp.int32)
     goes = jnp.sum(jnp.where(came[:, None] == ids[None, :], inference_slot[None, :], 0), axis=1)
-    chooser = (
-        (jnp.arange(rows)[:, None, None, None] + 4 * core == jnp.arange(16)[None, None, None, :])
-        & (ids[None, :, None, None] == goes[None, None, :, None])
-    ).astype(blocks[0].dtype).reshape(rows * slots, slots * 16)
     any_space = pl.BlockSpec(memory_space=pl.ANY)
     placed = pl.pallas_call(
         functools.partial(placing_kernel, slots),
         out_shape=jax.ShapeDtypeStruct((parts, rows, slots, width), blocks[0].dtype),
         in_specs=[
             pl.BlockSpec(memory_space=pltpu.SMEM),
-            pl.BlockSpec(memory_space=pltpu.VMEM),
+            pl.BlockSpec(memory_space=pltpu.SMEM),
         ]
         + [any_space] * slots,
         out_specs=pl.BlockSpec(memory_space=pltpu.HBM),
@@ -97,7 +101,7 @@
         compiler_params=pltpu.CompilerParams(vmem_limit_bytes=16 << 20),
         cost_estimate=pl.CostEstimate(flops=2 << 30, bytes_accessed=16 << 20, transcendentals=0),
         name="placing",
-    )(me[None].astype(jnp.int32), chooser, *blocks)
+    )(me[None].astype(jnp.int32), goes, *blocks)
     return jnp.transpose(placed, (2, 0, 1, 3))
 
 
@@ -309,12 +313,13 @@
     combine_matrix = jnp.dot(
         row_owner.T, placing * share.reshape(-1)[:, None], precision=lax.Precision.HIGHEST
     )
+    combine_matrix = passed_on(jnp.concatenate([combine_matrix] * Z_HI, axis=1))
     own_rows = lax.all_to_all(outgoing, "mp", split_axis=0, concat_axis=0, tiled=True)
     groups = rows_of_all(own_rows.reshape(-1, model_width))
     sums = []
-    for blocks in groups:
+    for turn, blocks in enumerate(groups):
         partials = expert_apply(blocks, expert_weights[0])
-        sums.append(sums_along_y(partials))
+        sums.append(lax.optimization_barrier(sums_along_y(partials)) if turn == 0 else sums_along_y(partials))
     first = lax.axis_index("dp") % Z_HI == 0
     answer = jnp.stack([jnp.where(first, sums[0], sums[1]), jnp.where(first, sums[1], sums[0])])
     answer = answer.reshape(Z_HI * mp_count, capacity, model_width)
@@ -326,7 +331,7 @@
         answer, ("dp", "mp"), 0, 0, axis_index_groups=teams, tiled=True
     )
     expert_mix = jnp.dot(
-        jnp.concatenate([combine_matrix] * Z_HI, axis=1),
+        combine_matrix,
         returned.reshape(-1, model_width).astype(jnp.float32),
         precision=lax.Precision.HIGHEST,
     ).astype(jnp.bfloat16)

time: 219 us -> 219 us (level)
  starting transfers between devices: 77.5 us -> 121 us
  waiting for transfers between devices: 80.3 us -> 38.2 us
  local copies, waits for them, and re-layouts: 23.7 us -> 20.5 us
  Pallas kernels: 25.1 us -> 27.4 us
    ppermute x7, waiting for transfers between devices: 32.6 us -> 0.02 us  [moved_experts(): blocks.append(lax.ppermute(block, 'mp', chip_pairs(*shift)))]
    ppermute x8, starting transfers between devices: 27.2 us -> 52.9 us  [moved_experts(): swapped.append(lax.ppermute(block, 'mp', CORE_PAIRS))]
    ppermute x7, starting transfers between devices: 7.28 us -> 15.6 us  [moved_experts(): blocks.append(lax.ppermute(block, 'mp', chip_pairs(*shift)))]
    ppermute x6, waiting for transfers between devices: 10.4 us -> 4.36 us  [rows_of_all(): groups[-1].append(lax.ppermute(block, 'dp', row_pairs(dy, 0)))]
    ppermute x6, waiting for transfers between devices: 14.4 us -> 9.1 us  [sums_along_y(): came.append(lax.ppermute(block, 'dp', row_pairs(-dy, 0)))]
    ppermute x6, starting transfers between devices: 5.72 us -> 10.1 us  [sums_along_y(): came.append(lax.ppermute(block, 'dp', row_pairs(-dy, 0)))]
    all_to_all x1, starting transfers between devices: 8.83 us -> 11.9 us  [handoff(): lax.all_to_all(answer, ('dp', 'mp'), 0, 0, axis_index_groups=teams, tiled...]
    ppermute x1, waiting for transfers between devices: 3.21 us -> 6.19 us  [rows_of_all(): other = lax.ppermute(own, 'dp', row_pairs(0, 1))]
  transfers between devices with their start and end apart: 32 -> 32, of which waited for: 16 -> 8; matrix products, arithmetic and copies ran while one was open for 8% -> 8% of each run, Pallas kernels for 12% -> 13%
where the time goes in v2:
time: 219 us; the launch traced here: 218 us
  starting transfers between devices  121 us (55%)
  waiting for transfers between devices  38.2 us (17%)
  Pallas kernels  27.4 us (13%)
  local copies, waits for them, and re-layouts  20.5 us (9%)
  other arithmetic  4.26 us (2%)
  between operations  3.99 us (2%)
  matrix products  2.58 us (1%)
    ppermute x8, starting transfers between devices, moved_experts(): swapped.append(lax.ppermute(block, 'mp', CORE_PAIRS))  52.9 us
    ppermute x7, starting transfers between devices, moved_experts(): blocks.append(lax.ppermute(block, 'mp', chip_pairs(*shift)))  15.6 us
    all_to_all x1, waiting for transfers between devices, handoff(): summed = lax.all_to_all(partial_value, ('dp', 'mp'), 0, 0, tiled=True)  13.7 us
    pallas_call x2, Pallas kernels, expert_apply(): pl.pallas_call(functools.partial(expert_kernel, count), out_shape=[jax.Sh...  12.9 us
    all_to_all x1, starting transfers between devices, handoff(): lax.all_to_all(answer, ('dp', 'mp'), 0, 0, axis_index_groups=teams, tiled...  11.9 us
    all_to_all x1, starting transfers between devices, handoff(): summed = lax.all_to_all(partial_value, ('dp', 'mp'), 0, 0, tiled=True)  10.4 us
    ppermute x6, starting transfers between devices, sums_along_y(): came.append(lax.ppermute(block, 'dp', row_pairs(-dy, 0)))  10.1 us
    ppermute x6, waiting for transfers between devices, sums_along_y(): came.append(lax.ppermute(block, 'dp', row_pairs(-dy, 0)))  9.1 us
  transfers between devices with their start and end apart: 32, of which 8 were waited for; matrix products, arithmetic and copies ran while one was open for 8% of the time, Pallas kernels for 13%

profile of v2, /device:TPU:1, one launch (start us, length us, event | category | flops | bytes accessed | tf_op | source)
XLA Modules:
  0.0 218.2 jit_solution(15958325783499291439)
XLA Ops:
  0.7 1.7 broadcast_in_dim.52
  2.4 8.5 %all-to-all-start = ((bf16[8,64,512]{2,1,0:T(8,128)(2,1)}), bf16[8,64,512]{2,1,0:T(8,128)(2,1)S(1)}, u32[]{:S(2)}, u32[]{:S(2)}) async-start(bf16[8,64,512]{2,1,0:T(8,128)(2,1)} %broadcast_in_dim.52), calls=%async_computation | async-start | bytes 1048576 | tf_op jit(solution)/shard_map/all_to_all | solution.py:272
  10.9 3.0 %dynamic-slice_bitcast_fusion = (bf16[3,24,5120]{2,1,0:T(8,128)(2,1)}, bf16[3,24,5120]{2,1,0:T(8,128)(2,1)}, bf16[3,24,5120]{2,1,0:T(8,128)(2,1)}) fusion(bf16[1,3,192,5120]{3,2,1,0:T(8,128)(2,1)} %param.13, s32[]{:T(128)S(6)} %select_n.241, s32[]{:T(128)S(6)} %select_n.236, s32[]{:T(128)S(6)} %select_n.238), kind=kLoop, calls=%fused_computation.9 | loop fusion | bytes 4423692 | tf_op jit(solution)/shard_map/dynamic_slice | solution.py:124
  13.9 1.2 collective-permute-start.13
  15.1 0.5 shard_map.105.source
  15.6 1.2 shard_map.106
  19.8 1.2 shard_map.107
  21.0 1.3 shard_map.103
  22.2 0.8 copy.11
  23.8 0.6 convolution_convert_fusion.2
  24.4 1.0 reshape.90
  25.4 10.4 %all-to-all-start.1 = ((bf16[128,4,640]{2,1,0:T(4,128)(2,1)}), bf16[128,4,640]{2,1,0:T(4,128)(2,1)S(1)}, u32[]{:S(2)}, u32[]{:S(2)}) async-start(bf16[128,4,640]{2,1,0:T(4,128)(2,1)} %reshape.90), calls=%async_computation.1 | async-start | bytes 1310720 | tf_op jit(solution)/shard_map/all_to_all | solution.py:281
  35.7 0.8 select_reduce_fusion.4.goes
  37.0 13.7 %all-to-all-done.1 = bf16[128,4,640]{2,1,0:T(4,128)(2,1)S(1)} async-done(((bf16[128,4,640]{2,1,0:T(4,128)(2,1)}), bf16[128,4,640]{2,1,0:T(4,128)(2,1)S(1)}, u32[]{:S(2)}, u32[]{:S(2)}) %all-to-all-start.1) | async-done | bytes 655392 | tf_op jit(solution)/shard_map/all_to_all | solution.py:281
  50.7 0.3 convert_reduce_fusion
  51.2 0.3 convolution_convert_fusion
  51.5 0.8 reshape.93
  52.3 4.3 %all-to-all-start.2 = ((bf16[16,2,5120]{2,1,0:T(2,128)(2,1)}), bf16[16,2,5120]{2,1,0:T(2,128)(2,1)S(1)}, u32[]{:S(2)}, u32[]{:S(2)}) async-start(bf16[16,2,5120]{2,1,0:T(2,128)(2,1)} %reshape.93), calls=%async_computation.2 | async-start | bytes 655360 | tf_op jit(solution)/shard_map/all_to_all | solution.py:317
  56.6 3.7 %constant_dynamic-slice_fusion.3 = (bf16[3,24,5120]{2,1,0:T(8,128)(2,1)}, bf16[3,24,5120]{2,1,0:T(8,128)(2,1)}, bf16[3,24,5120]{2,1,0:T(8,128)(2,1)}, bf16[3,24,5120]{2,1,0:T(8,128)(2,1)}, bf16[3,24,5120]{2,1,0:T(8,128)(2,1)S(1)}) fusion(bf16[3,192,5120]{2,1,0:T(8,128)(2,1)} %bitcast.46, s32[]{:T(128)S(6)} %select_n.246, s32[]{:T(128)S(6)} %select_n.245, ...), kind=kLoop, calls=%fused_computation.49 | loop fusion | bytes 7372820 | tf_op jit(solution)/shard_map/dynamic_slice | solution.py:124
  60.3 4.1 %all-to-all-done.2 = bf16[16,2,5120]{2,1,0:T(2,128)(2,1)S(1)} async-done(((bf16[16,2,5120]{2,1,0:T(2,128)(2,1)}), bf16[16,2,5120]{2,1,0:T(2,128)(2,1)S(1)}, u32[]{:S(2)}, u32[]{:S(2)}) %all-to-all-start.2) | async-done | bytes 327712 | tf_op jit(solution)/shard_map/all_to_all | solution.py:317
  64.5 0.5 collective-permute-start.6
  65.0 0.8 collective-permute-start.2
  65.9 1.9 collective-permute-start.1
  68.3 6.2 %collective-permute-done.6.refs_0_ = bf16[32,5120]{1,0:T(8,128)(2,1)S(1)} collective-permute-done((bf16[32,5120]{1,0:T(8,128)(2,1)S(1)}, bf16[32,5120]{1,0:T(8,128)(2,1)S(1)}, u32[]{:S(2)}, u32[]{:S(2)}) %collective-permute-start.6) | collective-permute-done | bytes 327712 | tf_op jit(solution)/shard_map/ppermute | solution.py:233
  74.4 2.4 %collective-permute-start.14 = (bf16[3,24,5120]{2,1,0:T(8,128)(2,1)}, bf16[3,24,5120]{2,1,0:T(8,128)(2,1)S(1)}, u32[]{:S(2)}, u32[]{:S(2)}) collective-permute-start(bf16[3,24,5120]{2,1,0:T(8,128)(2,1)} %get-tuple-element.31), channel_id=1, source_target_pairs={{0,6},{1,7},{2,0},{3,1},{4,2},{5,3},{6,4},{7,5},{8,14},{9,15},{10,... | collective-permute-start | bytes 2211848 | tf_op jit(solution)/shard_map/ppermute | solution.py:141
  76.8 0.5 collective-permute-start.9
  77.3 4.3 %collective-permute-done.1.refs_2_ = bf16[32,5120]{1,0:T(8,128)(2,1)S(1)} collective-permute-done((bf16[32,5120]{1,0:T(8,128)(2,1)S(1)}, bf16[32,5120]{1,0:T(8,128)(2,1)S(1)}, u32[]{:S(2)}, u32[]{:S(2)}) %collective-permute-start.1) | collective-permute-done | bytes 327712 | tf_op jit(solution)/shard_map/ppermute | solution.py:238
  81.7 3.9 %collective-permute-start.8 = (bf16[32,5120]{1,0:T(8,128)(2,1)S(1)}, bf16[32,5120]{1,0:T(8,128)(2,1)S(1)}, u32[]{:S(2)}, u32[]{:S(2)}) collective-permute-start(bf16[32,5120]{1,0:T(8,128)(2,1)S(1)} %collective-permute-done.6.refs_0_), channel_id=1, source_target_pairs={{0,96},{16,112},{32,0},{48,16},{64,32},{80,48},{96,64},{112,80},{1... | collective-permute-start | bytes 983048 | tf_op jit(solution)/shard_map/ppermute | solution.py:238
  85.6 0.7 copy-done.20
  86.3 6.5 %experts.2 = (bf16[32,5120]{1,0:T(8,128)(2,1)}, bf16[32,5120]{1,0:T(8,128)(2,1)}, bf16[32,5120]{1,0:T(8,128)(2,1)}, bf16[32,5120]{1,0:T(8,128)(2,1)}) custom-call(bf16[32,5120]{1,0:T(8,128)(2,1)} %copy-done.9, bf16[32,5120]{1,0:T(8,128)(2,1)} %copy-done.20, bf16[32,5120]{1,0:T(8,128)(2,1)} %copy-done.18, bf16[32,5120]{1,0:T(8,128)(2,1)} %copy-done.17, ...), custom_call_target="tpu_custom_call" | custom-call | flops 4294967296 | bytes 12582912 | tf_op jit(solution)/shard_map/experts/pallas_call | solution.py:206
  92.8 2.0 collective-permute-start.3
  94.8 2.8 %collective-permute-start.4 = (bf16[32,5120]{1,0:T(8,128)(2,1)}, bf16[32,5120]{1,0:T(8,128)(2,1)S(1)}, u32[]{:S(2)}, u32[]{:S(2)}) collective-permute-start(bf16[32,5120]{1,0:T(8,128)(2,1)} %get-tuple-element.23), channel_id=1, source_target_pairs={{0,32},{16,48},{32,64},{48,80},{64,96},{80,112},{96,0},{112,16},{1... | collective-permute-start | bytes 983048 | tf_op jit(solution)/shard_map/ppermute | solution.py:252
  97.7 0.7 copy-done.21
  98.4 1.2 collective-permute-start.5
  99.6 6.5 %experts.3 = (bf16[32,5120]{1,0:T(8,128)(2,1)}, bf16[32,5120]{1,0:T(8,128)(2,1)}, bf16[32,5120]{1,0:T(8,128)(2,1)}, bf16[32,5120]{1,0:T(8,128)(2,1)}) custom-call(bf16[32,5120]{1,0:T(8,128)(2,1)} %copy-done.15, bf16[32,5120]{1,0:T(8,128)(2,1)} %copy-done.21, bf16[32,5120]{1,0:T(8,128)(2,1)} %copy-done.19, bf16[32,5120]{1,0:T(8,128)(2,1)} %copy-done.16, ...), custom_call_target="tpu_custom_call" | custom-call | flops 4294967296 | bytes 12582912 | tf_op jit(solution)/shard_map/experts/pallas_call | solution.py:206
  106.1 2.0 collective-permute-start.10
  108.1 4.9 %collective-permute-done.5 = bf16[32,5120]{1,0:T(8,128)(2,1)S(1)} collective-permute-done((bf16[32,5120]{1,0:T(8,128)(2,1)}, bf16[32,5120]{1,0:T(8,128)(2,1)S(1)}, u32[]{:S(2)}, u32[]{:S(2)}) %collective-permute-start.5) | collective-permute-done | bytes 327712 | tf_op jit(solution)/shard_map/ppermute | solution.py:252
  113.0 2.1 collective-permute-start.12
  115.3 0.3 collective-permute-start.15
  115.6 2.0 collective-permute-done.11
  117.6 6.2 %collective-permute-start.16 = (bf16[3,24,5120]{2,1,0:T(8,128)(2,1)}, bf16[3,24,5120]{2,1,0:T(8,128)(2,1)}, u32[]{:S(2)}, u32[]{:S(2)}) collective-permute-start(bf16[3,24,5120]{2,1,0:T(8,128)(2,1)} %get-tuple-element.33), channel_id=1, source_target_pairs={{0,4},{1,5},{2,6},{3,7},{4,0},{5,1},{6,2},{7,3},{8,12},{9,13},{10,... | collective-permute-start | bytes 2211848 | tf_op jit(solution)/shard_map/ppermute | solution.py:141
  123.8 2.2 %collective-permute-done.12 = bf16[32,5120]{1,0:T(8,128)(2,1)S(1)} collective-permute-done((bf16[32,5120]{1,0:T(8,128)(2,1)}, bf16[32,5120]{1,0:T(8,128)(2,1)S(1)}, u32[]{:S(2)}, u32[]{:S(2)}) %collective-permute-start.12) | collective-permute-done | bytes 327712 | tf_op jit(solution)/shard_map/ppermute | solution.py:252
  126.0 2.0 collective-permute-start.17
  128.0 1.2 select_bitcast_fusion.1
  129.2 1.6 collective-permute-start.18
  130.8 1.8 collective-permute-start.19
  132.7 50.9 %collective-permute-start.20 = (bf16[3,24,5120]{2,1,0:T(8,128)(2,1)S(1)}, bf16[3,24,5120]{2,1,0:T(8,128)(2,1)S(1)}, u32[]{:S(2)}, u32[]{:S(2)}) collective-permute-start(bf16[3,24,5120]{2,1,0:T(8,128)(2,1)S(1)} %get-tuple-element.47.refs_0_), channel_id=1, source_target_pairs={{0,1},{1,0},{2,3},{3,2},{4,5},{5,4},{6,7},{7,6},{8,9},{9,8},{10,11... | collective-permute-start | bytes 2211848 | tf_op jit(solution)/shard_map/ppermute | solution.py:144
  183.6 0.5 collective-permute-start.22
  184.3 0.4 collective-permute-start.24
  184.8 0.7 collective-permute-done.20.refs_8_
  185.5 0.9 copy-done.1
  186.3 0.4 collective-permute-start.25
  186.7 0.9 copy-done.3
  187.8 0.9 copy-done.5
  188.8 0.3 collective-permute-start.27
  189.2 1.1 reshape.95
  190.2 11.9 %all-to-all-start.3 = ((bf16[32,2,5120]{2,1,0:T(2,128)(2,1)}), bf16[32,2,5120]{2,1,0:T(2,128)(2,1)S(1)}, u32[]{:S(2)}, u32[]{:S(2)}) async-start(bf16[32,2,5120]{2,1,0:T(2,128)(2,1)} %reshape.95), calls=%async_computation.3 | async-start | bytes 1310720 | tf_op jit(solution)/shard_map/all_to_all | solution.py:330
  202.6 0.7 pad_maximum_fusion.1.source
  203.3 1.3 shard_map.104
  204.6 1.1 copy-done.2
  205.7 1.1 copy-done.4
  206.8 1.1 copy-done.6
  207.9 9.0 %placing.1 = bf16[3,12,16,5120]{3,2,1,0:T(8,128)(2,1)} custom-call(s32[1]{0:T(128)} %bitcast.8.meta, s32[16]{0:T(128)S(1)} %select_reduce_fusion.4.goes, bf16[3,24,5120]{2,1,0:T(8,128)(2,1)S(1)} %get-tuple-element.47.refs_0_, bf16[3,24,5120]{2,1,0:T(8,128)(2,1)S(1)} %collective-permute-done.13.refs_1_, ...), custom_call_target="tpu_custom_call" | custom-call | flops 2147483648 | bytes 16777216 | tf_op jit(solution)/shard_map/placing/pallas_call | solution.py:86
  217.2 1.0 convolution_convert_fusion.1
  (93 shorter events, 3.4 us)
Async XLA Ops:
  0.6 23.2 %copy-start = (bf16[512,640]{1,0:T(8,128)(2,1)S(1)}, bf16[512,640]{1,0:T(8,128)(2,1)}, u32[]{:S(2)}) copy-start(bf16[512,640]{1,0:T(8,128)(2,1)} %param.9) | copy-start | bytes 1966084
  0.6 22.4 %copy-start.23 = (s32[16]{0:T(128)S(1)}, s32[16]{0:T(128)}, u32[]{:S(2)}) copy-start(s32[16]{0:T(128)} %param.14) | copy-start | bytes 196
  2.4 48.6 %copy-start.12 = (bf16[4,5120]{1,0:T(4,128)(2,1)S(1)}, bf16[4,5120]{1,0:T(4,128)(2,1)}, u32[]{:S(2)}) copy-start(bf16[4,5120]{1,0:T(4,128)(2,1)} %param.10) | copy-start | bytes 122884
  2.4 48.8 %copy-start.13 = (f32[5120]{0:T(1024)S(1)}, f32[5120]{0:T(1024)}, u32[]{:S(2)}) copy-start(f32[5120]{0:T(1024)} %param.11) | copy-start | bytes 61444
  2.4 21.4 %all-to-all-start = ((bf16[8,64,512]{2,1,0:T(8,128)(2,1)}), bf16[8,64,512]{2,1,0:T(8,128)(2,1)S(1)}, u32[]{:S(2)}, u32[]{:S(2)}) async-start(bf16[8,64,512]{2,1,0:T(8,128)(2,1)} %broadcast_in_dim.52), calls=%async_computation | async-start | bytes 1048576 | tf_op jit(solution)/shard_map/all_to_all | solution.py:272
  13.9 115.4 %collective-permute-start.13 = (bf16[3,24,5120]{2,1,0:T(8,128)(2,1)}, bf16[3,24,5120]{2,1,0:T(8,128)(2,1)S(1)}, u32[]{:S(2)}, u32[]{:S(2)}) collective-permute-start(bf16[3,24,5120]{2,1,0:T(8,128)(2,1)} %get-tuple-element.30), channel_id=1, source_target_pairs={{0,2},{1,3},{2,4},{3,5},{4,6},{5,7},{6,0},{7,1},{8,10},{9,11},{10,... | collective-permute-start | bytes 2211848 | tf_op jit(solution)/shard_map/ppermute | solution.py:141
  25.4 42.4 %copy-start.22 = (bf16[16,5120]{1,0:T(8,128)(2,1)S(1)}, bf16[16,5120]{1,0:T(8,128)(2,1)}, u32[]{:S(2)}) copy-start(bf16[16,5120]{1,0:T(8,128)(2,1)} %param.12) | copy-start | bytes 491524
  25.4 25.4 %all-to-all-start.1 = ((bf16[128,4,640]{2,1,0:T(4,128)(2,1)}), bf16[128,4,640]{2,1,0:T(4,128)(2,1)S(1)}, u32[]{:S(2)}, u32[]{:S(2)}) async-start(bf16[128,4,640]{2,1,0:T(4,128)(2,1)} %reshape.90), calls=%async_computation.1 | async-start | bytes 1310720 | tf_op jit(solution)/shard_map/all_to_all | solution.py:281
  51.2 17.1 %copy-start.11 = (bf16[4,5120]{1,0:T(4,128)(2,1)}, bf16[4,5120]{1,0:T(4,128)(2,1)S(1)}, u32[]{:S(2)}) copy-start(bf16[4,5120]{1,0:T(4,128)(2,1)S(1)} %get-tuple-element.42) | copy-start | bytes 122884
  52.3 12.0 %all-to-all-start.2 = ((bf16[16,2,5120]{2,1,0:T(2,128)(2,1)}), bf16[16,2,5120]{2,1,0:T(2,128)(2,1)S(1)}, u32[]{:S(2)}, u32[]{:S(2)}) async-start(bf16[16,2,5120]{2,1,0:T(2,128)(2,1)} %reshape.93), calls=%async_computation.2 | async-start | bytes 655360 | tf_op jit(solution)/shard_map/all_to_all | solution.py:317
  64.5 21.1 %copy-start.9 = (bf16[32,5120]{1,0:T(8,128)(2,1)}, bf16[32,5120]{1,0:T(8,128)(2,1)S(1)}, u32[]{:S(2)}) copy-start(bf16[32,5120]{1,0:T(8,128)(2,1)S(1)} %reshape.94.refs_0_) | copy-start | bytes 983044
  64.5 9.9 %collective-permute-start.6 = (bf16[32,5120]{1,0:T(8,128)(2,1)S(1)}, bf16[32,5120]{1,0:T(8,128)(2,1)S(1)}, u32[]{:S(2)}, u32[]{:S(2)}) collective-permute-start(bf16[32,5120]{1,0:T(8,128)(2,1)S(1)} %reshape.94.refs_0_), channel_id=1, source_target_pairs={{0,16},{16,0},{32,48},{48,32},{64,80},{80,64},{96,112},{112,96},{1... | collective-permute-start | bytes 983048 | tf_op jit(solution)/shard_map/ppermute | solution.py:233
  65.0 11.8 %collective-permute-start.2 = (bf16[32,5120]{1,0:T(8,128)(2,1)S(1)}, bf16[32,5120]{1,0:T(8,128)(2,1)S(1)}, u32[]{:S(2)}, u32[]{:S(2)}) collective-permute-start(bf16[32,5120]{1,0:T(8,128)(2,1)S(1)} %reshape.94.refs_0_), channel_id=1, source_target_pairs={{0,64},{16,80},{32,96},{48,112},{64,0},{80,16},{96,32},{112,48},{1... | collective-permute-start | bytes 983048 | tf_op jit(solution)/shard_map/ppermute | solution.py:238
  65.9 15.8 %collective-permute-start.1 = (bf16[32,5120]{1,0:T(8,128)(2,1)S(1)}, bf16[32,5120]{1,0:T(8,128)(2,1)S(1)}, u32[]{:S(2)}, u32[]{:S(2)}) collective-permute-start(bf16[32,5120]{1,0:T(8,128)(2,1)S(1)} %reshape.94.refs_0_), channel_id=1, source_target_pairs={{0,96},{16,112},{32,0},{48,16},{64,32},{80,48},{96,64},{112,80},{1... | collective-permute-start | bytes 983048 | tf_op jit(solution)/shard_map/ppermute | solution.py:238
  67.8 17.8 %collective-permute-start = (bf16[32,5120]{1,0:T(8,128)(2,1)S(1)}, bf16[32,5120]{1,0:T(8,128)(2,1)S(1)}, u32[]{:S(2)}, u32[]{:S(2)}) collective-permute-start(bf16[32,5120]{1,0:T(8,128)(2,1)S(1)} %reshape.94.refs_0_), channel_id=1, source_target_pairs={{0,32},{16,48},{32,64},{48,80},{64,96},{80,112},{96,0},{112,16},{1... | collective-permute-start | bytes 983048 | tf_op jit(solution)/shard_map/ppermute | solution.py:238
  74.4 18.4 %copy-start.15 = (bf16[32,5120]{1,0:T(8,128)(2,1)}, bf16[32,5120]{1,0:T(8,128)(2,1)S(1)}, u32[]{:S(2)}) copy-start(bf16[32,5120]{1,0:T(8,128)(2,1)S(1)} %collective-permute-done.6.refs_0_) | copy-start | bytes 983044
  74.4 56.4 %collective-permute-start.14 = (bf16[3,24,5120]{2,1,0:T(8,128)(2,1)}, bf16[3,24,5120]{2,1,0:T(8,128)(2,1)S(1)}, u32[]{:S(2)}, u32[]{:S(2)}) collective-permute-start(bf16[3,24,5120]{2,1,0:T(8,128)(2,1)} %get-tuple-element.31), channel_id=1, source_target_pairs={{0,6},{1,7},{2,0},{3,1},{4,2},{5,3},{6,4},{7,5},{8,14},{9,15},{10,... | collective-permute-start | bytes 2211848 | tf_op jit(solution)/shard_map/ppermute | solution.py:141
  76.8 8.8 %copy-start.17 = (bf16[32,5120]{1,0:T(8,128)(2,1)}, bf16[32,5120]{1,0:T(8,128)(2,1)S(1)}, u32[]{:S(2)}) copy-start(bf16[32,5120]{1,0:T(8,128)(2,1)S(1)} %collective-permute-done.2.refs_3_) | copy-start | bytes 983044
  76.8 16.0 %collective-permute-start.9 = (bf16[32,5120]{1,0:T(8,128)(2,1)S(1)}, bf16[32,5120]{1,0:T(8,128)(2,1)S(1)}, u32[]{:S(2)}, u32[]{:S(2)}) collective-permute-start(bf16[32,5120]{1,0:T(8,128)(2,1)S(1)} %collective-permute-done.6.refs_0_), channel_id=1, source_target_pairs={{0,64},{16,80},{32,96},{48,112},{64,0},{80,16},{96,32},{112,48},{1... | collective-permute-start | bytes 983048 | tf_op jit(solution)/shard_map/ppermute | solution.py:238
  81.7 3.9 %copy-start.18 = (bf16[32,5120]{1,0:T(8,128)(2,1)}, bf16[32,5120]{1,0:T(8,128)(2,1)S(1)}, u32[]{:S(2)}) copy-start(bf16[32,5120]{1,0:T(8,128)(2,1)S(1)} %collective-permute-done.1.refs_2_) | copy-start | bytes 983044
  81.7 13.2 %collective-permute-start.8 = (bf16[32,5120]{1,0:T(8,128)(2,1)S(1)}, bf16[32,5120]{1,0:T(8,128)(2,1)S(1)}, u32[]{:S(2)}, u32[]{:S(2)}) collective-permute-start(bf16[32,5120]{1,0:T(8,128)(2,1)S(1)} %collective-permute-done.6.refs_0_), channel_id=1, source_target_pairs={{0,96},{16,112},{32,0},{48,16},{64,32},{80,48},{96,64},{112,80},{1... | collective-permute-start | bytes 983048 | tf_op jit(solution)/shard_map/ppermute | solution.py:238
  85.6 0.8 copy-start.20
  85.6 12.1 %collective-permute-start.7 = (bf16[32,5120]{1,0:T(8,128)(2,1)S(1)}, bf16[32,5120]{1,0:T(8,128)(2,1)S(1)}, u32[]{:S(2)}, u32[]{:S(2)}) collective-permute-start(bf16[32,5120]{1,0:T(8,128)(2,1)S(1)} %collective-permute-done.6.refs_0_), channel_id=1, source_target_pairs={{0,32},{16,48},{32,64},{48,80},{64,96},{80,112},{96,0},{112,16},{1... | collective-permute-start | bytes 983048 | tf_op jit(solution)/shard_map/ppermute | solution.py:238
  92.8 4.8 %copy-start.16 = (bf16[32,5120]{1,0:T(8,128)(2,1)}, bf16[32,5120]{1,0:T(8,128)(2,1)S(1)}, u32[]{:S(2)}) copy-start(bf16[32,5120]{1,0:T(8,128)(2,1)S(1)} %collective-permute-done.9.refs_3_) | copy-start | bytes 983044
  92.8 13.3 %collective-permute-start.3 = (bf16[32,5120]{1,0:T(8,128)(2,1)}, bf16[32,5120]{1,0:T(8,128)(2,1)S(1)}, u32[]{:S(2)}, u32[]{:S(2)}) collective-permute-start(bf16[32,5120]{1,0:T(8,128)(2,1)} %get-tuple-element.22), channel_id=1, source_target_pairs={{0,96},{16,112},{32,0},{48,16},{64,32},{80,48},{96,64},{112,80},{1... | collective-permute-start | bytes 983048 | tf_op jit(solution)/shard_map/ppermute | solution.py:252
  94.8 2.8 %copy-start.19 = (bf16[32,5120]{1,0:T(8,128)(2,1)}, bf16[32,5120]{1,0:T(8,128)(2,1)S(1)}, u32[]{:S(2)}) copy-start(bf16[32,5120]{1,0:T(8,128)(2,1)S(1)} %collective-permute-done.8.refs_2_) | copy-start | bytes 983044
  94.8 13.3 %collective-permute-start.4 = (bf16[32,5120]{1,0:T(8,128)(2,1)}, bf16[32,5120]{1,0:T(8,128)(2,1)S(1)}, u32[]{:S(2)}, u32[]{:S(2)}) collective-permute-start(bf16[32,5120]{1,0:T(8,128)(2,1)} %get-tuple-element.23), channel_id=1, source_target_pairs={{0,32},{16,48},{32,64},{48,80},{64,96},{80,112},{96,0},{112,16},{1... | collective-permute-start | bytes 983048 | tf_op jit(solution)/shard_map/ppermute | solution.py:252
  97.7 0.7 copy-start.21
  98.4 16.7 %copy-start.10 = (bf16[32,5120]{1,0:T(8,128)(2,1)S(1)}, bf16[32,5120]{1,0:T(8,128)(2,1)}, u32[]{:S(2)}) copy-start(bf16[32,5120]{1,0:T(8,128)(2,1)} %get-tuple-element.21) | copy-start | bytes 983044
  98.4 16.9 %copy-start.7 = (bf16[3,24,5120]{2,1,0:T(8,128)(2,1)S(1)}, bf16[3,24,5120]{2,1,0:T(8,128)(2,1)}, u32[]{:S(2)}) copy-start(bf16[3,24,5120]{2,1,0:T(8,128)(2,1)} %get-tuple-element.32) | copy-start | bytes 2211844
  98.4 27.6 %copy-start.8 = (bf16[3,24,5120]{2,1,0:T(8,128)(2,1)S(1)}, bf16[3,24,5120]{2,1,0:T(8,128)(2,1)}, u32[]{:S(2)}) copy-start(bf16[3,24,5120]{2,1,0:T(8,128)(2,1)} %get-tuple-element.34) | copy-start | bytes 2211844
  98.4 14.6 %collective-permute-start.5 = (bf16[32,5120]{1,0:T(8,128)(2,1)}, bf16[32,5120]{1,0:T(8,128)(2,1)S(1)}, u32[]{:S(2)}, u32[]{:S(2)}) collective-permute-start(bf16[32,5120]{1,0:T(8,128)(2,1)} %get-tuple-element.24), channel_id=1, source_target_pairs={{0,64},{16,80},{32,96},{48,112},{64,0},{80,16},{96,32},{112,48},{1... | collective-permute-start | bytes 983048 | tf_op jit(solution)/shard_map/ppermute | solution.py:252
  106.1 9.2 %collective-permute-start.10 = (bf16[32,5120]{1,0:T(8,128)(2,1)}, bf16[32,5120]{1,0:T(8,128)(2,1)S(1)}, u32[]{:S(2)}, u32[]{:S(2)}) collective-permute-start(bf16[32,5120]{1,0:T(8,128)(2,1)} %get-tuple-element.26), channel_id=1, source_target_pairs={{0,96},{16,112},{32,0},{48,16},{64,32},{80,48},{96,64},{112,80},{1... | collective-permute-start | bytes 983048 | tf_op jit(solution)/shard_map/ppermute | solution.py:252
  108.1 9.5 %collective-permute-start.11 = (bf16[32,5120]{1,0:T(8,128)(2,1)}, bf16[32,5120]{1,0:T(8,128)(2,1)S(1)}, u32[]{:S(2)}, u32[]{:S(2)}) collective-permute-start(bf16[32,5120]{1,0:T(8,128)(2,1)} %get-tuple-element.27), channel_id=1, source_target_pairs={{0,32},{16,48},{32,64},{48,80},{64,96},{80,112},{96,0},{112,16},{1... | collective-permute-start | bytes 983048 | tf_op jit(solution)/shard_map/ppermute | solution.py:252
  113.0 13.0 %collective-permute-start.12 = (bf16[32,5120]{1,0:T(8,128)(2,1)}, bf16[32,5120]{1,0:T(8,128)(2,1)S(1)}, u32[]{:S(2)}, u32[]{:S(2)}) collective-permute-start(bf16[32,5120]{1,0:T(8,128)(2,1)} %get-tuple-element.28), channel_id=1, source_target_pairs={{0,64},{16,80},{32,96},{48,112},{64,0},{80,16},{96,32},{112,48},{1... | collective-permute-start | bytes 983048 | tf_op jit(solution)/shard_map/ppermute | solution.py:252
  115.3 17.4 %collective-permute-start.15 = (bf16[3,24,5120]{2,1,0:T(8,128)(2,1)S(1)}, bf16[3,24,5120]{2,1,0:T(8,128)(2,1)}, u32[]{:S(2)}, u32[]{:S(2)}) collective-permute-start(bf16[3,24,5120]{2,1,0:T(8,128)(2,1)S(1)} %copy-done.7), channel_id=1, source_target_pairs={{0,8},{1,9},{2,10},{3,11},{4,12},{5,13},{6,14},{7,15},{8,0},{9,1},... | collective-permute-start | bytes 2211848 | tf_op jit(solution)/shard_map/ppermute | solution.py:141
  117.6 66.0 %collective-permute-start.16 = (bf16[3,24,5120]{2,1,0:T(8,128)(2,1)}, bf16[3,24,5120]{2,1,0:T(8,128)(2,1)}, u32[]{:S(2)}, u32[]{:S(2)}) collective-permute-start(bf16[3,24,5120]{2,1,0:T(8,128)(2,1)} %get-tuple-element.33), channel_id=1, source_target_pairs={{0,4},{1,5},{2,6},{3,7},{4,0},{5,1},{6,2},{7,3},{8,12},{9,13},{10,... | collective-permute-start | bytes 2211848 | tf_op jit(solution)/shard_map/ppermute | solution.py:141
  126.0 57.6 %collective-permute-start.17 = (bf16[3,24,5120]{2,1,0:T(8,128)(2,1)S(1)}, bf16[3,24,5120]{2,1,0:T(8,128)(2,1)}, u32[]{:S(2)}, u32[]{:S(2)}) collective-permute-start(bf16[3,24,5120]{2,1,0:T(8,128)(2,1)S(1)} %copy-done.8), channel_id=1, source_target_pairs={{0,10},{1,11},{2,12},{3,13},{4,14},{5,15},{6,8},{7,9},{8,2},{9,3},... | collective-permute-start | bytes 2211848 | tf_op jit(solution)/shard_map/ppermute | solution.py:141
  129.2 54.9 %collective-permute-start.18 = (bf16[3,24,5120]{2,1,0:T(8,128)(2,1)}, bf16[3,24,5120]{2,1,0:T(8,128)(2,1)}, u32[]{:S(2)}, u32[]{:S(2)}) collective-permute-start(bf16[3,24,5120]{2,1,0:T(8,128)(2,1)} %get-tuple-element.35), channel_id=1, source_target_pairs={{0,14},{1,15},{2,8},{3,9},{4,10},{5,11},{6,12},{7,13},{8,6},{9,7},... | collective-permute-start | bytes 2211848 | tf_op jit(solution)/shard_map/ppermute | solution.py:141
  130.8 53.5 %collective-permute-start.19 = (bf16[3,24,5120]{2,1,0:T(8,128)(2,1)}, bf16[3,24,5120]{2,1,0:T(8,128)(2,1)}, u32[]{:S(2)}, u32[]{:S(2)}) collective-permute-start(bf16[3,24,5120]{2,1,0:T(8,128)(2,1)} %get-tuple-element.36), channel_id=1, source_target_pairs={{0,12},{1,13},{2,14},{3,15},{4,8},{5,9},{6,10},{7,11},{8,4},{9,5},... | collective-permute-start | bytes 2211848 | tf_op jit(solution)/shard_map/ppermute | solution.py:141
  132.7 52.8 %collective-permute-start.20 = (bf16[3,24,5120]{2,1,0:T(8,128)(2,1)S(1)}, bf16[3,24,5120]{2,1,0:T(8,128)(2,1)S(1)}, u32[]{:S(2)}, u32[]{:S(2)}) collective-permute-start(bf16[3,24,5120]{2,1,0:T(8,128)(2,1)S(1)} %get-tuple-element.47.refs_0_), channel_id=1, source_target_pairs={{0,1},{1,0},{2,3},{3,2},{4,5},{5,4},{6,7},{7,6},{8,9},{9,8},{10,11... | collective-permute-start | bytes 2211848 | tf_op jit(solution)/shard_map/ppermute | solution.py:144
  183.6 3.1 %collective-permute-start.21 = (bf16[3,24,5120]{2,1,0:T(8,128)(2,1)S(1)}, bf16[3,24,5120]{2,1,0:T(8,128)(2,1)S(1)}, u32[]{:S(2)}, u32[]{:S(2)}) collective-permute-start(bf16[3,24,5120]{2,1,0:T(8,128)(2,1)S(1)} %collective-permute-done.13.refs_1_), channel_id=1, source_target_pairs={{0,1},{1,0},{2,3},{3,2},{4,5},{5,4},{6,7},{7,6},{8,9},{9,8},{10,11... | collective-permute-start | bytes 2211848 | tf_op jit(solution)/shard_map/ppermute | solution.py:144
  183.6 4.2 %collective-permute-start.22 = (bf16[3,24,5120]{2,1,0:T(8,128)(2,1)S(1)}, bf16[3,24,5120]{2,1,0:T(8,128)(2,1)S(1)}, u32[]{:S(2)}, u32[]{:S(2)}) collective-permute-start(bf16[3,24,5120]{2,1,0:T(8,128)(2,1)S(1)} %collective-permute-done.14.refs_2_), channel_id=1, source_target_pairs={{0,1},{1,0},{2,3},{3,2},{4,5},{5,4},{6,7},{7,6},{8,9},{9,8},{10,11... | collective-permute-start | bytes 2211848 | tf_op jit(solution)/shard_map/ppermute | solution.py:144
  184.2 20.3 %collective-permute-start.23 = (bf16[3,24,5120]{2,1,0:T(8,128)(2,1)}, bf16[3,24,5120]{2,1,0:T(8,128)(2,1)}, u32[]{:S(2)}, u32[]{:S(2)}) collective-permute-start(bf16[3,24,5120]{2,1,0:T(8,128)(2,1)} %collective-permute-done.15.refs_3_), channel_id=1, source_target_pairs={{0,1},{1,0},{2,3},{3,2},{4,5},{5,4},{6,7},{7,6},{8,9},{9,8},{10,11... | collective-permute-start | bytes 2211848 | tf_op jit(solution)/shard_map/ppermute | solution.py:144
  184.3 20.2 %collective-permute-start.24 = (bf16[3,24,5120]{2,1,0:T(8,128)(2,1)}, bf16[3,24,5120]{2,1,0:T(8,128)(2,1)}, u32[]{:S(2)}, u32[]{:S(2)}) collective-permute-start(bf16[3,24,5120]{2,1,0:T(8,128)(2,1)} %collective-permute-done.16.refs_4_), channel_id=1, source_target_pairs={{0,1},{1,0},{2,3},{3,2},{4,5},{5,4},{6,7},{7,6},{8,9},{9,8},{10,11... | collective-permute-start | bytes 2211848 | tf_op jit(solution)/shard_map/ppermute | solution.py:144
  185.5 0.9 copy-start.1
  186.3 18.2 %collective-permute-start.25 = (bf16[3,24,5120]{2,1,0:T(8,128)(2,1)}, bf16[3,24,5120]{2,1,0:T(8,128)(2,1)}, u32[]{:S(2)}, u32[]{:S(2)}) collective-permute-start(bf16[3,24,5120]{2,1,0:T(8,128)(2,1)} %collective-permute-done.17.refs_5_), channel_id=1, source_target_pairs={{0,1},{1,0},{2,3},{3,2},{4,5},{5,4},{6,7},{7,6},{8,9},{9,8},{10,11... | collective-permute-start | bytes 2211848 | tf_op jit(solution)/shard_map/ppermute | solution.py:144
  186.7 0.9 copy-start.3
  187.6 16.9 %collective-permute-start.26 = (bf16[3,24,5120]{2,1,0:T(8,128)(2,1)}, bf16[3,24,5120]{2,1,0:T(8,128)(2,1)}, u32[]{:S(2)}, u32[]{:S(2)}) collective-permute-start(bf16[3,24,5120]{2,1,0:T(8,128)(2,1)} %collective-permute-done.18.refs_6_), channel_id=1, source_target_pairs={{0,1},{1,0},{2,3},{3,2},{4,5},{5,4},{6,7},{7,6},{8,9},{9,8},{10,11... | collective-permute-start | bytes 2211848 | tf_op jit(solution)/shard_map/ppermute | solution.py:144
  187.8 0.9 copy-start.5
  188.8 15.8 %collective-permute-start.27 = (bf16[3,24,5120]{2,1,0:T(8,128)(2,1)}, bf16[3,24,5120]{2,1,0:T(8,128)(2,1)}, u32[]{:S(2)}, u32[]{:S(2)}) collective-permute-start(bf16[3,24,5120]{2,1,0:T(8,128)(2,1)} %collective-permute-done.19.refs_7_), channel_id=1, source_target_pairs={{0,1},{1,0},{2,3},{3,2},{4,5},{5,4},{6,7},{7,6},{8,9},{9,8},{10,11... | collective-permute-start | bytes 2211848 | tf_op jit(solution)/shard_map/ppermute | solution.py:144
  190.2 26.7 %all-to-all-start.3 = ((bf16[32,2,5120]{2,1,0:T(2,128)(2,1)}), bf16[32,2,5120]{2,1,0:T(2,128)(2,1)S(1)}, u32[]{:S(2)}, u32[]{:S(2)}) async-start(bf16[32,2,5120]{2,1,0:T(2,128)(2,1)} %reshape.95), calls=%async_computation.3 | async-start | bytes 1310720 | tf_op jit(solution)/shard_map/all_to_all | solution.py:330
  204.6 1.1 copy-start.2
  205.7 1.1 copy-start.4
  206.8 1.1 copy-start.6
  207.9 9.3 %copy-start.14 = (f32[4,64]{1,0:T(4,128)S(1)}, f32[4,64]{1,0:T(4,128)}, u32[]{:S(2)}) copy-start(f32[4,64]{1,0:T(4,128)} %shard_map.104) | copy-start | bytes 3076
